TPU v7x, 512 devices: a whole 4x4x16 slice. The times are simulated.
512 devices in a mesh: rows: 128 (over z, y, core), help: 4 (over x).
Axes of the slice: x: 4, y: 4, z: 16, core: 2. Of those that a mesh axis runs over, the one named last changes fastest.
Arguments:
- embeddings: float32 [131072, 768], P(('rows', 'help')), may hold values from -40 to 40
- cluster_ids: int32 [131072], P(('rows', 'help')), may hold values from 0 to 511, as said below
- orders: int32 [131072], P(('rows', 'help')), may hold values from 0 to 1023, as said below
- owner: int32 [512], replicated, may hold values from 0 to 511, each once
Outputs:
- centroids: float32 [512, 768], P(('rows', 'help'))
- max_cosine: float32 [131072], P(('rows', 'help'))
- center_cosine: float32 [131072], P(('rows', 'help'))
Inputs may be any that keep to these rules, and one draw needn't show every extreme that they name: `cluster_ids`: among the 256 rows of one device no cluster appears more than 2 times; one cluster appears exactly 2 times on every device; every cluster has at least one row. Within each cluster the orders of its rows are distinct and run from 0 to its number of rows minus 1. `owner`: each device index appears exactly once.
All inputs are finite; a program needn't handle non-finite values.
Results may differ from a plain program's by a relative error of at most 0.007.
Values may be sent and summed in bfloat16 or wider, within the bound.
No kernel may reach another device: no remote copies, remote signals or barrier semaphores. Data moves between devices by JAX's collectives and lax.ppermute only.
A program may use at most 64 MiB of HBM per device.

v0:
```python
import jax
import jax.numpy as jnp
from jax import lax
from jax.sharding import PartitionSpec as P


def unit_rows(matrix):
    squares = jnp.sum(matrix * matrix, axis=-1, keepdims=True)
    return (matrix * lax.rsqrt(squares + 1e-06)).astype(jnp.bfloat16)


def scale_rows(matrix):
    squares = jnp.sum(matrix * matrix, axis=-1)
    return jnp.sqrt(squares + 1e-06).astype(jnp.bfloat16)


def local(embeddings, cluster_ids, orders, owner):
    rows_dev = embeddings.shape[0]
    features = embeddings.shape[1]
    row_groups = lax.axis_size("rows")
    help_groups = lax.axis_size("help")
    groups = row_groups * help_groups
    capacity = 4 * rows_dev // groups
    slot_count = groups * capacity
    cluster_hot = cluster_ids[:, None] == jnp.arange(groups, dtype=jnp.int32)[None, :]
    target = jnp.sum(jnp.where(cluster_hot, owner[None, :], 0), axis=1)
    target_hot = target[:, None] == jnp.arange(groups, dtype=jnp.int32)[None, :]
    row_index = jnp.arange(rows_dev, dtype=jnp.int32)
    same_before = (target[None, :] == target[:, None]) & (row_index[None, :] < row_index[:, None])
    slot_rank = jnp.sum(same_before.astype(jnp.int32), axis=1)
    slot_index = target * capacity + slot_rank
    slot_source = jnp.full((slot_count,), rows_dev, jnp.int32).at[slot_index].set(row_index)
    padded_orders = jnp.concatenate([orders, jnp.full((1,), -1, jnp.int32)])
    send_orders = padded_orders[slot_source].reshape(row_groups, help_groups, capacity)
    units = unit_rows(embeddings)
    rebuilt = units.astype(jnp.float32) * scale_rows(embeddings).astype(jnp.float32)[:, None]
    hot_float = target_hot.astype(jnp.float32)
    center_sum = lax.psum_scatter(
        lax.dot_general(
            hot_float,
            rebuilt,
            (((0,), (0,)), ((), ())),
            precision=lax.Precision.HIGHEST,
            preferred_element_type=jnp.float32,
        ),
        ("rows", "help"),
        scatter_dimension=0,
        tiled=True,
    )[0]
    padded_units = jnp.concatenate([units, jnp.zeros((1, features), jnp.bfloat16)])
    send_units = padded_units[slot_source].reshape(row_groups, help_groups, capacity, features)
    got_units, got_orders = (
        lax.all_to_all(
            lax.all_to_all(send_units, "rows", split_axis=0, concat_axis=0, tiled=True),
            "help",
            split_axis=1,
            concat_axis=1,
            tiled=True,
        ),
        lax.all_to_all(
            lax.all_to_all(send_orders, "rows", split_axis=0, concat_axis=0, tiled=True),
            "help",
            split_axis=1,
            concat_axis=1,
            tiled=True,
        ),
    )
    key_units = got_units.reshape(slot_count, features)
    key_orders = got_orders.reshape(slot_count)
    filled = key_orders >= 0
    members = jnp.sum(filled.astype(jnp.float32))
    center = center_sum / members
    direction = (center * lax.rsqrt(jnp.sum(center * center) + 1e-06)).astype(jnp.bfloat16)
    aligned = jnp.dot(key_units, direction, preferred_element_type=jnp.float32)
    query_blocks = key_units.reshape(slot_count // 512, 512, features)
    query_orders = key_orders.reshape(slot_count // 512, 512)

    def best_earlier(block_pair):
        queries, orders_here = block_pair
        scores = lax.dot_general(
            queries, key_units, (((1,), (1,)), ((), ())), preferred_element_type=jnp.float32
        )
        earlier_mask = filled[None, :] & (key_orders[None, :] < orders_here[:, None])
        return jnp.max(jnp.where(earlier_mask, scores, -1.0), axis=1)

    nearest = lax.map(best_earlier, (query_blocks, query_orders)).reshape(slot_count)
    back_nearest, back_aligned = (
        lax.all_to_all(
            lax.all_to_all(
                nearest.reshape(row_groups, help_groups, capacity),
                "rows",
                split_axis=0,
                concat_axis=0,
                tiled=True,
            ),
            "help",
            split_axis=1,
            concat_axis=1,
            tiled=True,
        ),
        lax.all_to_all(
            lax.all_to_all(
                aligned.reshape(row_groups, help_groups, capacity),
                "rows",
                split_axis=0,
                concat_axis=0,
                tiled=True,
            ),
            "help",
            split_axis=1,
            concat_axis=1,
            tiled=True,
        ),
    )
    max_cosine = back_nearest.reshape(slot_count)[slot_index]
    center_cosine = back_aligned.reshape(slot_count)[slot_index]
    return (center.reshape(1, features), max_cosine, center_cosine)


def solution(mesh):
    return jax.shard_map(
        local,
        mesh=mesh,
        in_specs=(P(("rows", "help"), None), P(("rows", "help")), P(("rows", "help")), P()),
        out_specs=(P(("rows", "help"), None), P(("rows", "help")), P(("rows", "help"))),
        check_vma=False,
    )
```

profile of v0, /device:TPU:1, one launch (start us, length us, event | category | flops | bytes accessed | tf_op | source)
XLA Modules:
  0.0 718.7 jit_solution(849735388457465759)
XLA Ops:
  7.2 0.9 select_reduce_fusion.1
  8.1 0.2 convert_reduce_fusion
  8.3 1.4 scatter_custom_fusion
  9.7 0.7 pad_add_fusion
  10.4 0.0 copy-start
  10.4 6.9 gather_fusion
  17.3 0.3 reshape.77
  17.6 1.5 copy.45
  19.1 20.6 %all-to-all-start = ((s32[128,4,2]{1,2,0:T(2,128)}), s32[128,4,2]{1,2,0:T(2,128)S(1)}, u32[]{:S(2)}, u32[]{:S(2)}) async-start(s32[128,4,2]{1,2,0:T(2,128)} %copy.45), calls=%async_computation | async-start | bytes 262144 | tf_op jit(solution)/shard_map/all_to_all | solution.py:61
  39.6 0.0 copy-done
  39.7 0.1 multiply_reduce_fusion
  39.8 0.1 multiply_convert_fusion
  40.0 4.0 gather_fusion.1
  44.0 1.5 reshape.78
  45.5 10.1 %all-to-all-done = s32[128,4,2]{1,2,0:T(2,128)S(1)} async-done(((s32[128,4,2]{1,2,0:T(2,128)}), s32[128,4,2]{1,2,0:T(2,128)S(1)}, u32[]{:S(2)}, u32[]{:S(2)}) %all-to-all-start) | async-done | bytes 4128 | tf_op jit(solution)/shard_map/all_to_all | solution.py:61
  55.6 7.2 %all-to-all-start.2 = ((bf16[128,4,2,768]{3,2,1,0:T(2,128)(2,1)}), bf16[128,4,2,768]{3,2,1,0:T(2,128)(2,1)S(1)}, u32[]{:S(2)}, u32[]{:S(2)}) async-start(bf16[128,4,2,768]{3,2,1,0:T(2,128)(2,1)} %reshape.78), calls=%async_computation.2 | async-start | bytes 3145728 | tf_op jit(solution)/shard_map/all_to_all | solution.py:54
  62.8 0.7 copy.46
  63.5 72.3 %all-to-all-done.2 = bf16[128,4,2,768]{3,2,1,0:T(2,128)(2,1)S(1)} async-done(((bf16[128,4,2,768]{3,2,1,0:T(2,128)(2,1)}), bf16[128,4,2,768]{3,2,1,0:T(2,128)(2,1)S(1)}, u32[]{:S(2)}, u32[]{:S(2)}) %all-to-all-start.2) | async-done | bytes 1572896 | tf_op jit(solution)/shard_map/all_to_all | solution.py:54
  135.8 4.0 all-to-all-start.1
  139.8 2.2 copy.49
  142.1 1.9 all-to-all-done.1
  144.0 3.6 all-to-all-start.3
  147.6 0.2 all-reduce.4.cloned.1.call-start
  147.8 2.3 fusion.5
  150.0 0.0 all-reduce.4.cloned.1.call-update
  150.1 0.2 copy.52
  150.3 0.0 copy-start.1
  150.3 0.2 reshape_reshape.9
  150.5 0.2 lt.76
  150.8 0.6 convert_reduce_fusion.1
  151.4 0.2 copy.47
  151.6 0.2 ge.8
  151.8 478.3 %all-reduce.4.cloned.1.call-done = f32[512,768]{1,0:T(8,128)} async-done(((f32[512,768]{1,0:T(8,128)}), f32[512,768]{1,0:T(8,128)}) %all-reduce.4.cloned.1.call-update) | async-done | bytes 1572880
  630.0 2.0 multiply_reduce_fusion.1
  632.7 0.0 all-to-all-done.3
  632.7 1.1 copy.50
  633.8 0.0 copy-done.1
  633.8 1.5 reshape.79
  635.4 1.5 reshape_reshape.10
  636.9 0.0 copy-done.3
  636.9 0.5 fusion.3
  637.4 0.8 copy.60
  638.2 15.2 %all-to-all-start.6 = ((f32[128,4,2]{1,2,0:T(2,128)}), f32[128,4,2]{1,2,0:T(2,128)S(1)}, u32[]{:S(2)}, u32[]{:S(2)}) async-start(f32[128,4,2]{1,2,0:T(2,128)} %bitcast.6), calls=%async_computation.6 | async-start | bytes 262144 | tf_op jit(solution)/shard_map/all_to_all | solution.py:102
  653.4 0.0 copy-done.2
  653.4 4.8 while.11
  653.4 2.3 select_reduce_fusion.4
  655.8 2.3 select_reduce_fusion.4
  658.2 0.3 reshape_reshape.11
  658.5 1.5 copy.53
  660.0 9.4 %all-to-all-done.6 = f32[128,4,2]{1,2,0:T(2,128)S(1)} async-done(((f32[128,4,2]{1,2,0:T(2,128)}), f32[128,4,2]{1,2,0:T(2,128)S(1)}, u32[]{:S(2)}, u32[]{:S(2)}) %all-to-all-start.6) | async-done | bytes 4128 | tf_op jit(solution)/shard_map/all_to_all | solution.py:102
  669.4 7.2 %all-to-all-start.4 = ((f32[128,4,2]{1,2,0:T(2,128)}), f32[128,4,2]{1,2,0:T(2,128)S(1)}, u32[]{:S(2)}, u32[]{:S(2)}) async-start(f32[128,4,2]{1,2,0:T(2,128)} %copy.53), calls=%async_computation.4 | async-start | bytes 262144 | tf_op jit(solution)/shard_map/all_to_all | solution.py:89
  676.6 0.7 copy.56
  677.3 15.3 %all-to-all-done.4 = f32[128,4,2]{1,2,0:T(2,128)S(1)} async-done(((f32[128,4,2]{1,2,0:T(2,128)}), f32[128,4,2]{1,2,0:T(2,128)S(1)}, u32[]{:S(2)}, u32[]{:S(2)}) %all-to-all-start.4) | async-done | bytes 4128 | tf_op jit(solution)/shard_map/all_to_all | solution.py:89
  692.6 3.5 all-to-all-start.7
  696.1 0.7 copy.54
  696.8 3.5 all-to-all-done.7
  700.3 3.2 all-to-all-start.5
  703.5 0.2 copy.57
  703.7 0.2 reshape.81
  703.9 3.7 all-to-all-done.5
  707.6 0.2 copy.55
  707.8 0.2 reshape.80
  708.0 1.9 gather_fusion.3
  709.9 1.9 gather_fusion.2
  (14 shorter events, 0.2 us)
Async XLA Ops:
  10.4 29.3 %copy-start = (f32[256,768]{1,0:T(8,128)S(1)}, f32[256,768]{1,0:T(8,128)}, u32[]{:S(2)}) copy-start(f32[256,768]{1,0:T(8,128)} %param.6) | copy-start | bytes 2359300
  19.1 36.5 %all-to-all-start = ((s32[128,4,2]{1,2,0:T(2,128)}), s32[128,4,2]{1,2,0:T(2,128)S(1)}, u32[]{:S(2)}, u32[]{:S(2)}) async-start(s32[128,4,2]{1,2,0:T(2,128)} %copy.45), calls=%async_computation | async-start | bytes 262144 | tf_op jit(solution)/shard_map/all_to_all | solution.py:61
  55.6 80.2 %all-to-all-start.2 = ((bf16[128,4,2,768]{3,2,1,0:T(2,128)(2,1)}), bf16[128,4,2,768]{3,2,1,0:T(2,128)(2,1)S(1)}, u32[]{:S(2)}, u32[]{:S(2)}) async-start(bf16[128,4,2,768]{3,2,1,0:T(2,128)(2,1)} %reshape.78), calls=%async_computation.2 | async-start | bytes 3145728 | tf_op jit(solution)/shard_map/all_to_all | solution.py:54
  135.8 8.2 %all-to-all-start.1 = ((s32[128,4,2]{0,2,1:T(2,128)}), s32[128,4,2]{0,2,1:T(2,128)S(1)}, u32[]{:S(2)}, u32[]{:S(2)}) async-start(s32[128,4,2]{0,2,1:T(2,128)} %copy.46), calls=%async_computation.1 | async-start | bytes 8192 | tf_op jit(solution)/shard_map/all_to_all | solution.py:60
  144.0 488.7 %all-to-all-start.3 = ((bf16[128,4,2,768]{3,2,0,1:T(2,128)(2,1)}), bf16[128,4,2,768]{3,2,0,1:T(2,128)(2,1)S(1)}, u32[]{:S(2)}, u32[]{:S(2)}) async-start(bf16[128,4,2,768]{3,2,0,1:T(2,128)(2,1)} %copy.49), calls=%async_computation.3 | async-start | bytes 3145728 | tf_op jit(solution)/shard_map/all_to_all | solution.py:53
  147.6 482.5 %all-reduce.4.cloned.1.call-start = ((), (), s32[]{:S(2)}) async-start(), calls=%async_computation.8 | async-start | bytes 3145728
  150.3 483.6 %copy-start.1 = (s32[128,4,2]{2,1,0:T(4,128)}, s32[128,4,2]{2,1,0:T(4,128)S(1)}, u32[]{:S(2)}) copy-start(s32[128,4,2]{2,1,0:T(4,128)S(1)} %copy.52) | copy-start | bytes 12292
  632.0 4.8 copy-start.3
  636.8 16.6 %copy-start.2 = (bf16[1024,768]{1,0:T(8,128)(2,1)S(1)}, bf16[1024,768]{1,0:T(8,128)(2,1)}, u32[]{:S(2)}) copy-start(bf16[1024,768]{1,0:T(8,128)(2,1)} %reshape.79) | copy-start | bytes 4718596
  638.2 31.2 %all-to-all-start.6 = ((f32[128,4,2]{1,2,0:T(2,128)}), f32[128,4,2]{1,2,0:T(2,128)S(1)}, u32[]{:S(2)}, u32[]{:S(2)}) async-start(f32[128,4,2]{1,2,0:T(2,128)} %bitcast.6), calls=%async_computation.6 | async-start | bytes 262144 | tf_op jit(solution)/shard_map/all_to_all | solution.py:102
  669.4 23.2 %all-to-all-start.4 = ((f32[128,4,2]{1,2,0:T(2,128)}), f32[128,4,2]{1,2,0:T(2,128)S(1)}, u32[]{:S(2)}, u32[]{:S(2)}) async-start(f32[128,4,2]{1,2,0:T(2,128)} %copy.53), calls=%async_computation.4 | async-start | bytes 262144 | tf_op jit(solution)/shard_map/all_to_all | solution.py:89
  692.6 7.7 %all-to-all-start.7 = ((f32[128,4,2]{0,2,1:T(2,128)}), f32[128,4,2]{0,2,1:T(2,128)S(1)}, u32[]{:S(2)}, u32[]{:S(2)}) async-start(f32[128,4,2]{0,2,1:T(2,128)} %copy.56), calls=%async_computation.7 | async-start | bytes 8192 | tf_op jit(solution)/shard_map/all_to_all | solution.py:101
  700.3 7.3 %all-to-all-start.5 = ((f32[128,4,2]{0,2,1:T(2,128)}), f32[128,4,2]{0,2,1:T(2,128)S(1)}, u32[]{:S(2)}, u32[]{:S(2)}) async-start(f32[128,4,2]{0,2,1:T(2,128)} %copy.54), calls=%async_computation.5 | async-start | bytes 8192 | tf_op jit(solution)/shard_map/all_to_all | solution.py:88
Sparse Core Ops, SparseCore 0:
  153.7 476.2 all-reduce.3
where the time goes:
time: 722 us; the launch traced here: 719 us
  waiting for transfers between devices  594 us (82%)
  starting transfers between devices  64.7 us (9%)
  local copies, waits for them, and re-layouts  32.5 us (5%)
  between operations  15 us (2%)
  matrix products  7.37 us (1%)
    unnamed x2, waiting for transfers between devices  478 us
    all_to_all x1, waiting for transfers between devices, local(): lax.all_to_all(send_units, 'rows', split_axis=0, concat_axis=0, tiled=True)  72.3 us
    all_to_all x1, starting transfers between devices, local(): lax.all_to_all(send_orders, 'rows', split_axis=0, concat_axis=0, tiled=True)  20.6 us
    all_to_all x1, waiting for transfers between devices, local(): lax.all_to_all(nearest.reshape(row_groups, help_groups, capacity), 'rows'...  15.3 us
    all_to_all x1, starting transfers between devices, local(): lax.all_to_all(aligned.reshape(row_groups, help_groups, capacity), 'rows'...  15.2 us
  transfers between devices with their start and end apart: 9, of which 8 were waited for; matrix products, arithmetic and copies ran while one was open for 3% of the time, Pallas kernels for 0%

commit v1 on v0

v1 whole, which is shorter than its diff:
```python
import jax
import jax.numpy as jnp
from jax import lax
from jax.experimental import pallas as pl
from jax.experimental.pallas import tpu as pltpu
from jax.sharding import Mesh
from jax.sharding import PartitionSpec as P

ALL = ("z", "y", "core", "x")
SLAB = ("y", "core", "x")
NZ = 16
NQ = 32
DEVS = NZ * NQ
ROWS = 256
D = 768
W = D + 128
BF = jnp.bfloat16
F32 = jnp.float32
NT = (((1,), (1,)), ((), ()))
TN = (((0,), (0,)), ((), ()))


def column(row):
    return jnp.transpose(jnp.broadcast_to(row, (128, row.shape[1])))[:, :1]


def call(kernel, shapes, *args):
    return pl.pallas_call(
        kernel,
        out_shape=shapes,
        in_specs=[pl.BlockSpec(memory_space=pltpu.VMEM) for _ in args],
        out_specs=[pl.BlockSpec(memory_space=pltpu.VMEM) for _ in shapes],
    )(*args)


def targets(ids_row, owner_row):
    hot = (lax.broadcasted_iota(jnp.int32, (DEVS, ROWS), 0) == ids_row).astype(F32).astype(BF)
    high = owner_row // 16
    low = owner_row - high * 16
    sub = lax.broadcasted_iota(jnp.int32, (8, DEVS), 0)
    digits = jnp.where(sub == 0, high, jnp.where(sub == 1, low, 0)).astype(F32).astype(BF)
    found = jnp.dot(digits, hot, preferred_element_type=F32)
    return found[0:1] * 16.0 + found[1:2]


def rank_among_equal(row):
    col = column(row)
    j = lax.broadcasted_iota(jnp.int32, (ROWS, ROWS), 0)
    i = lax.broadcasted_iota(jnp.int32, (ROWS, ROWS), 1)
    return jnp.sum(jnp.where((col == row) & (j < i), 1.0, 0.0), axis=0, keepdims=True)


def pack_kernel(emb_ref, ids_ref, ord_ref, own_ref, out_ref, slot_ref):
    target = targets(ids_ref[...], own_ref[...])
    rank = rank_among_equal(target)
    pos = (rank * DEVS + target).astype(jnp.int32)
    slot_ref[...] = pos
    emb = emb_ref[...]
    squares = jnp.sum(emb * emb, axis=1, keepdims=True) + 1e-06
    units = (emb * lax.rsqrt(squares)).astype(BF)
    scale = jnp.sqrt(squares).astype(BF)
    lane = lax.broadcasted_iota(jnp.int32, (ROWS, 128), 1)
    scale_lanes = jnp.where(lane == 0, scale.astype(F32), 0.0).astype(BF)
    order = ord_ref[...]
    high = order // 256
    low = order - high * 256
    sub = lax.broadcasted_iota(jnp.int32, (128, ROWS), 0)
    order_lanes = jnp.where(sub == 1, high + 1, jnp.where(sub == 2, low, 0)).astype(F32).astype(BF)
    for k in range(2):
        place = (lax.broadcasted_iota(jnp.int32, (DEVS, ROWS), 0) + k * DEVS == pos).astype(F32).astype(BF)
        rows = pl.ds(k * DEVS, DEVS)
        out_ref[rows, :D] = jnp.dot(place, units, preferred_element_type=F32).astype(BF)
        meta = jnp.dot(place, scale_lanes, preferred_element_type=F32)
        meta = meta + lax.dot_general(place, order_lanes, NT, preferred_element_type=F32)
        out_ref[rows, D:] = meta.astype(BF)


def owner_kernel(rows_ref, center_ref, back_ref):
    total = 2 * DEVS
    meta = rows_ref[:, D:].astype(F32)
    meta_t = jnp.transpose(meta)
    order_col = (meta[:, 1:2] - 1.0) * 256.0 + meta[:, 2:3]
    key_col = jnp.where(order_col >= 0.0, order_col, 1e6)
    order_row = (meta_t[1:2] - 1.0) * 256.0 + meta_t[2:3]
    members = jnp.sum(jnp.where(order_row >= 0.0, 1.0, 0.0))
    keys = rows_ref[:, :D]
    scale = jnp.broadcast_to(meta_t[0:1], (8, total)).astype(BF)
    center = jnp.dot(scale, keys, preferred_element_type=F32)[0:1] / members
    center_ref[...] = center
    length = lax.rsqrt(jnp.sum(center * center, axis=1, keepdims=True) + 1e-06)
    direction = jnp.broadcast_to(center * length, (8, D)).astype(BF)
    aligned = lax.dot_general(direction, keys, NT, preferred_element_type=F32)[0:1]
    back_ref[2:3] = aligned[:, :DEVS]
    back_ref[3:4] = aligned[:, DEVS:]
    block = 256
    for b in range(total // block):
        scores = lax.dot_general(
            keys, rows_ref[pl.ds(b * block, block), :D], NT, preferred_element_type=F32
        )
        earlier = key_col < order_row[:, b * block : (b + 1) * block]
        best = jnp.max(jnp.where(earlier, scores, -1.0), axis=0, keepdims=True)
        k, first = divmod(b * block, DEVS)
        back_ref[k : k + 1, first : first + block] = best


def unpack_kernel(got_ref, slot_ref, near_ref, align_ref):
    slot = slot_ref[...]
    rank = slot // DEVS
    target = slot - rank * DEVS
    z = target // NQ
    q = target - z * NQ
    hot = (lax.broadcasted_iota(jnp.int32, (NQ, ROWS), 0) == q).astype(F32)
    column_of = lax.dot_general(
        got_ref[...], hot, TN, precision=lax.Precision.HIGHEST, preferred_element_type=F32
    )
    sub = lax.broadcasted_iota(jnp.int32, (NZ * 4, ROWS), 0)
    near_ref[...] = jnp.sum(jnp.where(sub == z * 4 + rank, column_of, 0.0), axis=0, keepdims=True)
    align_ref[...] = jnp.sum(jnp.where(sub == z * 4 + rank + 2, column_of, 0.0), axis=0, keepdims=True)


def local(embeddings, cluster_ids, orders, owner):
    sds = jax.ShapeDtypeStruct
    packed, slot = call(
        pack_kernel,
        [sds((2 * DEVS, W), BF), sds((1, ROWS), jnp.int32)],
        embeddings,
        cluster_ids.reshape(1, ROWS),
        orders.reshape(1, ROWS),
        owner.reshape(1, DEVS),
    )
    send = packed.reshape(2, DEVS, W).transpose(1, 0, 2)
    got = lax.all_to_all(send, ALL, split_axis=0, concat_axis=0, tiled=True)
    rows = got.transpose(1, 0, 2).reshape(2 * DEVS, W)
    center, back = call(owner_kernel, [sds((1, D), F32), sds((4, DEVS), F32)], rows)
    back = back.reshape(4, NZ, NQ).transpose(1, 0, 2).reshape(NZ, 1, 4 * NQ)
    back = lax.all_to_all(back, "z", split_axis=0, concat_axis=0, tiled=True)
    back = back.reshape(NZ, 4, NQ).transpose(2, 0, 1).reshape(NQ, 1, NZ * 4)
    back = lax.all_to_all(back, SLAB, split_axis=0, concat_axis=0, tiled=True)
    near, align = call(
        unpack_kernel,
        [sds((1, ROWS), F32), sds((1, ROWS), F32)],
        back.reshape(NQ, NZ * 4),
        slot,
    )
    return (center, near.reshape(ROWS), align.reshape(ROWS))


def solution(mesh):
    fine = Mesh(mesh.devices.reshape(16, 4, 2, 4), ALL)
    return jax.shard_map(
        local,
        mesh=fine,
        in_specs=(P(ALL, None), P(ALL), P(ALL), P()),
        out_specs=(P(ALL, None), P(ALL), P(ALL)),
        check_vma=False,
    )
```

time: 722 us -> 160 us (0.22)
  waiting for transfers between devices: 594 us -> 0 us
  blocking collectives: 0 us -> 142 us
  starting transfers between devices: 64.7 us -> 0 us
  local copies, waits for them, and re-layouts: 32.5 us -> 6.41 us
  between operations: 15 us -> 0.65 us
  Pallas kernels: 0 us -> 10.1 us
  matrix products: 7.37 us -> 0 us
    unnamed x2 -> x0, waiting for transfers between devices: 478 us -> none
    all_to_all x0 -> x3, blocking collectives: none -> 142 us  [the longest x1 116 us: local(): got = lax.all_to_all(send, ALL, split_axis=0, concat_axis=0, tiled=True)]
    all_to_all x8 -> x0, waiting for transfers between devices: 116 us -> none  [the longest x1 72.3 us: local(): lax.all_to_all(send_units, 'rows', split_axis=0, concat_axis=0, tiled=True)]
    all_to_all x8 -> x0, starting transfers between devices: 64.5 us -> none  [the longest x1 20.6 us: local(): lax.all_to_all(send_orders, 'rows', split_axis=0, concat_axis=0, tiled=True)]
    gather x4 -> x0, local copies, waits for them, and re-layouts: 14.7 us -> none  [the longest x1 6.86 us: local(): padded_orders[slot_source].reshape(row_groups, help_groups, capacity)]
    pallas_call x0 -> x3, Pallas kernels: none -> 10.1 us  [call(): pl.pallas_call(kernel, out_shape=shapes, in_specs=[pl.BlockSpec(memory_sp...]
    dot_general x4 -> x0, matrix products: 7.37 us -> none  [the longest x2 4.62 us: best_earlier(): lax.dot_general(queries, key_units, (((1,), (1,)), ((), ())), preferred_e...]
  transfers between devices with their start and end apart: 9 -> 0, of which waited for: 8 -> 0; matrix products, arithmetic and copies ran while one was open for 3% -> 0% of each run, Pallas kernels for 0% -> 0%
where the time goes in v1:
time: 160 us
  blocking collectives  142 us (89%)
  Pallas kernels  10.1 us (6%)
  local copies, waits for them, and re-layouts  6.41 us (4%)
    all_to_all x1, blocking collectives, local(): got = lax.all_to_all(send, ALL, split_axis=0, concat_axis=0, tiled=True)  116 us
    all_to_all x1, blocking collectives, local(): back = lax.all_to_all(back, 'z', split_axis=0, concat_axis=0, tiled=True)  13.8 us
    all_to_all x1, blocking collectives, local(): back = lax.all_to_all(back, SLAB, split_axis=0, concat_axis=0, tiled=True)  12.1 us
    pallas_call x3, Pallas kernels, call(): pl.pallas_call(kernel, out_shape=shapes, in_specs=[pl.BlockSpec(memory_sp...  10.1 us
    reshape x1, local copies, waits for them, and re-layouts, local(): send = packed.reshape(2, DEVS, W).transpose(1, 0, 2)  3.39 us

profile of v1, /device:TPU:1, one launch (start us, length us, event | category | flops | bytes accessed | tf_op | source)
XLA Modules:
  0.0 160.0 jit_solution(9779179255269004710)
XLA Ops:
  0.6 3.7 %shard_map.67 = (bf16[1024,896]{1,0:T(8,128)(2,1)}, s32[1,256]{1,0:T(1,128)}) custom-call(f32[256,768]{1,0:T(8,128)} %emb_ref.1, s32[1,256]{1,0:T(1,128)} %bitcast.28, s32[1,256]{1,0:T(1,128)} %bitcast.29, s32[1,512]{1,0:T(1,128)} %bitcast.27), custom_call_target="tpu_custom_call" | custom-call | tf_op jit(solution)/shard_map/pallas_call | solution.py:28
  4.3 3.4 %copy.16 = bf16[2,512,896]{2,0,1:T(2,128)(2,1)S(1)} copy(bf16[2,512,896]{2,1,0:T(8,128)(2,1)} %bitcast.22) | data formatting | bytes 3670016 | tf_op jit(solution)/shard_map/reshape | solution.py:131
  7.7 116.2 %all_to_all.15 = bf16[512,2,896]{2,1,0:T(2,128)(2,1)S(1)} all-to-all(bf16[512,2,896]{2,1,0:T(2,128)(2,1)S(1)} %bitcast.20), channel_id=1, replica_groups=mesh['z'=16,'y'=4,'core'=2,'x'=4] {'z','y','core','x'}, dimensions={0} | all-to-all | bytes 3670016 | tf_op jit(solution)/shard_map/all_to_all | solution.py:132
  123.9 1.5 copy.10
  125.4 4.9 %shard_map.68 = (f32[1,768]{1,0:T(1,128)}, f32[4,512]{1,0:T(4,128)}) custom-call(bf16[1024,896]{1,0:T(8,128)(2,1)} %bitcast.19), custom_call_target="tpu_custom_call" | custom-call | tf_op jit(solution)/shard_map/pallas_call | solution.py:28
  130.3 0.8 reshape.47
  131.1 0.1 reshape.48
  131.1 13.8 %all_to_all.16 = f32[16,1,128]{2,1,0:T(1,128)S(1)} all-to-all(f32[16,1,128]{2,1,0:T(1,128)S(1)} %bitcast.26), channel_id=1, replica_groups=mesh['z'=16,'y'=4,'core'=2,'x'=4] {'z'}, dimensions={0} | all-to-all | bytes 16384 | tf_op jit(solution)/shard_map/all_to_all | solution.py:136
  145.0 0.5 broadcast.3
  145.5 0.7 reduce.3
  146.2 0.1 reshape.49
  146.2 0.1 copy.13
  146.3 12.1 %all_to_all.17 = f32[32,1,64]{2,1,0:T(1,128)} all-to-all(f32[32,1,64]{2,1,0:T(1,128)S(1)} %copy.13), channel_id=1, replica_groups=mesh['z'=16,'y'=4,'core'=2,'x'=4] {'y','core','x'}, dimensions={0} | all-to-all | bytes 16384 | tf_op jit(solution)/shard_map/all_to_all | solution.py:138
  158.4 1.6 shard_map.69
  (1 shorter events, 0.0 us)

commit v2 on v1

--- a/solution.py
+++ b/solution.py
@@ -18,16 +18,22 @@
 F32 = jnp.float32
 NT = (((1,), (1,)), ((), ()))
 TN = (((0,), (0,)), ((), ()))
+STRIDE = 40
+FIT = STRIDE - 1
+SENT = NZ * STRIDE
+COLS = D // 128
+CHUNK = COLS * NQ + 8
 
 
 def column(row):
     return jnp.transpose(jnp.broadcast_to(row, (128, row.shape[1])))[:, :1]
 
 
-def call(kernel, shapes, *args):
+def call(kernel, shapes, *args, scratch=()):
     return pl.pallas_call(
         kernel,
         out_shape=shapes,
+        scratch_shapes=scratch,
         in_specs=[pl.BlockSpec(memory_space=pltpu.VMEM) for _ in args],
         out_specs=[pl.BlockSpec(memory_space=pltpu.VMEM) for _ in shapes],
     )(*args)
@@ -103,43 +109,186 @@
         back_ref[k : k + 1, first : first + block] = best
 
 
+def row_of(col):
+    return jnp.transpose(jnp.broadcast_to(col, (col.shape[0], 128)))[:1]
+
+
+def iota(shape, dim):
+    return lax.broadcasted_iota(jnp.int32, shape, dim)
+
+
+def hot(condition):
+    return condition.astype(F32).astype(BF)
+
+
+def dot(a, b):
+    return jnp.dot(a, b, preferred_element_type=F32)
+
+
+def dot_nt(a, b):
+    return lax.dot_general(a, b, NT, preferred_element_type=F32)
+
+
+def slab_pack_kernel(emb_ref, ids_ref, ord_ref, own_ref, out_ref, slot_ref):
+    target = targets(ids_ref[...], own_ref[...])
+    rank = rank_among_equal(target).astype(jnp.int32)
+    whole = target.astype(jnp.int32)
+    slot_ref[...] = rank * DEVS + whole
+    z = whole // NQ
+    q = whole - z * NQ
+    place = rank_among_equal(z.astype(F32)).astype(jnp.int32)
+    overflow = jnp.max((place >= FIT).astype(F32), axis=1, keepdims=True)
+    pos = jnp.where(place < FIT, z * STRIDE + place, -1)
+    emb = emb_ref[...]
+    squares = jnp.sum(emb * emb, axis=1, keepdims=True) + 1e-06
+    units = (emb * lax.rsqrt(squares)).astype(BF)
+    scale = row_of(jnp.sqrt(squares).astype(BF).astype(F32))
+    order = ord_ref[...]
+    high = order // 256
+    low = order - high * 256
+    sub = iota((NZ * 4, ROWS), 0)
+    value = sub // NZ
+    picked = jnp.where(
+        value == 0,
+        scale,
+        jnp.where(value == 1, high, jnp.where(value == 2, low, q * 2 + rank + 1)).astype(F32),
+    )
+    mine = jnp.where(sub - value * NZ == z, picked, 0.0).astype(BF)
+    found = dot_nt(mine, hot(iota((128, ROWS), 0) == place)).astype(BF)
+    flag = jnp.broadcast_to(overflow, (NZ, 128)).astype(BF)
+    meta = jnp.concatenate(
+        [found[v * NZ : (v + 1) * NZ] for v in range(4)] + [flag, jnp.zeros((NZ, 128), BF)], axis=1
+    )
+    spread = hot(iota((SENT, ROWS), 0) == pos)
+    last = hot(iota((SENT, NZ), 0) == iota((SENT, NZ), 1) * STRIDE + FIT)
+    out_ref[...] = (dot(spread, units) + dot(last, meta)).astype(BF)
+
+
+def repack_kernel(rows_ref, out_ref):
+    last = hot(iota((NZ, SENT), 1) == iota((NZ, SENT), 0) * STRIDE + FIT)
+    meta = dot(last, rows_ref[:, :640])
+    flag = jnp.max(meta[:, 512:640])
+    stacked = jnp.concatenate([meta[:, v * 128 : (v + 1) * 128] for v in range(4)], axis=0).astype(BF)
+    k = iota((128, SENT), 1)
+    along = dot(stacked, hot(iota((128, SENT), 0) == k - (k // STRIDE) * STRIDE))
+    sub = iota((NZ * 4, SENT), 0)
+    here = sub - (sub // NZ) * NZ == iota((NZ * 4, SENT), 1) // STRIDE
+    values = jnp.sum(jnp.where(here, along, 0.0).reshape(4, NZ, SENT), axis=1)
+    code = values[3:4].astype(jnp.int32) - 1
+    q = jnp.where(code >= 0, code // 2, -1)
+    rank = code - q * 2
+    slot = jnp.where(code >= 0, rank * NZ + iota((1, SENT), 1) // STRIDE, -1)
+    pos = jnp.where(code >= 0, q * NQ + slot, -1)
+    spread = hot(iota((2 * DEVS, SENT), 0) == pos)
+    moved = dot(spread, rows_ref[...]).astype(BF)
+    for c in range(COLS):
+        out_ref[:, c * NQ : (c + 1) * NQ, :] = moved[:, c * 128 : (c + 1) * 128].reshape(NQ, NQ, 128)
+    v = iota((8, SENT), 0)
+    filled = jnp.where(v == 3, 1.0, 0.0)
+    eight = jnp.where(v == 0, values[0:1], jnp.where(v == 1, values[1:2], jnp.where(v == 2, values[2:3], filled)))
+    eight = jnp.broadcast_to(eight[None], (NQ, 8, SENT)).reshape(NQ * 8, SENT)
+    mine = jnp.where(iota((NQ * 8, SENT), 0) // 8 == q, eight, 0.0).astype(BF)
+    details = dot_nt(mine, hot(iota((128, SENT), 0) == slot))
+    sub = iota((NQ * 8, 128), 0)
+    details = details + jnp.where(sub - (sub // 8) * 8 == 4, flag, 0.0)
+    out_ref[:, COLS * NQ :, :] = details.astype(BF).reshape(NQ, 8, 128)
+
+
+def slab_owner_kernel(rows_ref, center_ref, back_ref, flag_ref, keys_ref):
+    total = 2 * DEVS
+    for c in range(COLS):
+        keys_ref[:, c * 128 : (c + 1) * 128] = rows_ref[:, c * NQ : (c + 1) * NQ, :].reshape(total, 128)
+    details = rows_ref[:, COLS * NQ :, :].reshape(NQ * 8, 128)
+    n = iota((128, total), 1)
+    along = dot(details, hot(iota((128, total), 0) == n - (n // NQ) * NQ))
+    here = iota((NQ * 8, total), 0) // 8 == iota((NQ * 8, total), 1) // NQ
+    values = jnp.sum(jnp.where(here, along, 0.0).reshape(NQ, 8, total), axis=0)
+    flag_ref[...] = jnp.broadcast_to(jnp.max(values[4:5], axis=1, keepdims=True), (1, 128))
+    order_row = values[1:2] * 256.0 + values[2:3]
+    members = jnp.sum(values[3:4], axis=1, keepdims=True)
+    key_col = column(jnp.where(values[3:4] > 0.0, order_row, 1e6))
+    scale = jnp.broadcast_to(values[0:1], (8, total)).astype(BF)
+    center = dot(scale, keys_ref[...])[0:1] / members
+    center_ref[...] = center
+    length = lax.rsqrt(jnp.sum(center * center, axis=1, keepdims=True) + 1e-06)
+    direction = jnp.broadcast_to(center * length, (8, D)).astype(BF)
+    back_ref[1:2] = dot_nt(direction, keys_ref[...])[0:1]
+    block = 256
+    for b in range(total // block):
+        some = slice(b * block, (b + 1) * block)
+        scores = dot_nt(keys_ref[...], keys_ref[some, :])
+        back_ref[0:1, some] = jnp.max(
+            jnp.where(key_col < order_row[:, some], scores, -1.0), axis=0, keepdims=True
+        )
+
+
 def unpack_kernel(got_ref, slot_ref, near_ref, align_ref):
     slot = slot_ref[...]
     rank = slot // DEVS
     target = slot - rank * DEVS
     z = target // NQ
     q = target - z * NQ
-    hot = (lax.broadcasted_iota(jnp.int32, (NQ, ROWS), 0) == q).astype(F32)
+    from_z = (iota((NZ, ROWS), 0) == z).astype(F32)
     column_of = lax.dot_general(
-        got_ref[...], hot, TN, precision=lax.Precision.HIGHEST, preferred_element_type=F32
-    )
-    sub = lax.broadcasted_iota(jnp.int32, (NZ * 4, ROWS), 0)
-    near_ref[...] = jnp.sum(jnp.where(sub == z * 4 + rank, column_of, 0.0), axis=0, keepdims=True)
-    align_ref[...] = jnp.sum(jnp.where(sub == z * 4 + rank + 2, column_of, 0.0), axis=0, keepdims=True)
-
-
-def local(embeddings, cluster_ids, orders, owner):
+        got_ref[...], from_z, TN, precision=lax.Precision.HIGHEST, preferred_element_type=F32
+    )
+    sub = iota((128, ROWS), 0)
+    near_ref[...] = jnp.sum(jnp.where(sub == rank * NQ + q, column_of, 0.0), axis=0, keepdims=True)
+    align_ref[...] = jnp.sum(jnp.where(sub == (rank + 2) * NQ + q, column_of, 0.0), axis=0, keepdims=True)
+
+
+def full_exchange(embeddings, ids_row, orders_row, owner_row):
     sds = jax.ShapeDtypeStruct
-    packed, slot = call(
+    packed, _ = call(
         pack_kernel,
         [sds((2 * DEVS, W), BF), sds((1, ROWS), jnp.int32)],
         embeddings,
-        cluster_ids.reshape(1, ROWS),
-        orders.reshape(1, ROWS),
-        owner.reshape(1, DEVS),
+        ids_row,
+        orders_row,
+        owner_row,
     )
     send = packed.reshape(2, DEVS, W).transpose(1, 0, 2)
     got = lax.all_to_all(send, ALL, split_axis=0, concat_axis=0, tiled=True)
     rows = got.transpose(1, 0, 2).reshape(2 * DEVS, W)
     center, back = call(owner_kernel, [sds((1, D), F32), sds((4, DEVS), F32)], rows)
-    back = back.reshape(4, NZ, NQ).transpose(1, 0, 2).reshape(NZ, 1, 4 * NQ)
+    return center, back.reshape(2, 2, NZ, NQ).transpose(0, 3, 1, 2).reshape(2, 2 * DEVS)
+
+
+def local(embeddings, cluster_ids, orders, owner):
+    sds = jax.ShapeDtypeStruct
+    ids_row = cluster_ids.reshape(1, ROWS)
+    orders_row = orders.reshape(1, ROWS)
+    owner_row = owner.reshape(1, DEVS)
+    packed, slot = call(
+        slab_pack_kernel,
+        [sds((SENT, D), BF), sds((1, ROWS), jnp.int32)],
+        embeddings,
+        ids_row,
+        orders_row,
+        owner_row,
+    )
+    got = lax.all_to_all(packed.reshape(NZ, STRIDE, D), "z", split_axis=0, concat_axis=0, tiled=True)
+    (moved,) = call(repack_kernel, [sds((NQ, CHUNK, 128), BF)], got.reshape(SENT, D))
+    rows = lax.all_to_all(moved, SLAB, split_axis=0, concat_axis=0, tiled=True)
+    center, back, flag = call(
+        slab_owner_kernel,
+        [sds((1, D), F32), sds((2, 2 * DEVS), F32), sds((1, 128), F32)],
+        rows,
+        scratch=[pltpu.VMEM((2 * DEVS, D), BF)],
+    )
+    center, back = lax.cond(
+        flag[0, 0] > 0.0,
+        lambda: full_exchange(embeddings, ids_row, orders_row, owner_row),
+        lambda: (center, back),
+    )
+    back = back.reshape(2, NQ, NQ).transpose(1, 0, 2).reshape(NQ, 1, 2 * NQ)
+    back = lax.all_to_all(back, SLAB, split_axis=0, concat_axis=0, tiled=True)
+    back = back.reshape(NQ, 4, NZ).transpose(2, 1, 0).reshape(NZ, 1, 4 * NQ)
     back = lax.all_to_all(back, "z", split_axis=0, concat_axis=0, tiled=True)
-    back = back.reshape(NZ, 4, NQ).transpose(2, 0, 1).reshape(NQ, 1, NZ * 4)
-    back = lax.all_to_all(back, SLAB, split_axis=0, concat_axis=0, tiled=True)
     near, align = call(
         unpack_kernel,
         [sds((1, ROWS), F32), sds((1, ROWS), F32)],
-        back.reshape(NQ, NZ * 4),
+        back.reshape(NZ, 4 * NQ),
         slot,
     )
     return (center, near.reshape(ROWS), align.reshape(ROWS))

time: 160 us -> 141 us (0.88)
  blocking collectives: 142 us -> 87.7 us
  waiting for transfers between devices: 0 us -> 22.1 us
  starting transfers between devices: 0 us -> 14.3 us
  local copies, waits for them, and re-layouts: 6.41 us -> 1.58 us
  Pallas kernels: 10.1 us -> 13.6 us
    all_to_all x1, blocking collectives: 116 us -> 59.1 us  [local(): lax.all_to_all(packed.reshape(NZ, STRIDE, D), 'z', split_axis=0, concat_a...]
    all_to_all x0 -> x1, waiting for transfers between devices: none -> 22.1 us  [local(): rows = lax.all_to_all(moved, SLAB, split_axis=0, concat_axis=0, tiled=True)]
    all_to_all x0 -> x1, starting transfers between devices: none -> 14.3 us  [local(): rows = lax.all_to_all(moved, SLAB, split_axis=0, concat_axis=0, tiled=True)]
    reshape x6 -> x4, local copies, waits for them, and re-layouts: 4.41 us -> 0.28 us  [the longest x3 0.2 us: local(): back = back.reshape(2, NQ, NQ).transpose(1, 0, 2).reshape(NQ, 1, 2 * NQ)]
    pallas_call x3 -> x4, Pallas kernels: 10.1 us -> 13.6 us  [call(): pl.pallas_call(kernel, out_shape=shapes, scratch_shapes=scratch, in_specs...]
    all_to_all x1, blocking collectives: 13.8 us -> 16.4 us  [local(): back = lax.all_to_all(back, 'z', split_axis=0, concat_axis=0, tiled=True)]
  transfers between devices with their start and end apart: 0 -> 1, of which waited for: 0 -> 1; matrix products, arithmetic and copies ran while one was open for 0% -> 0% of each run, Pallas kernels for 0% -> 0%
where the time goes in v2:
time: 141 us
  blocking collectives  87.7 us (62%)
  waiting for transfers between devices  22.1 us (16%)
  starting transfers between devices  14.3 us (10%)
  Pallas kernels  13.6 us (10%)
  local copies, waits for them, and re-layouts  1.58 us (1%)
    all_to_all x1, blocking collectives, local(): lax.all_to_all(packed.reshape(NZ, STRIDE, D), 'z', split_axis=0, concat_a...  59.1 us
    all_to_all x1, waiting for transfers between devices, local(): rows = lax.all_to_all(moved, SLAB, split_axis=0, concat_axis=0, tiled=True)  22.1 us
    all_to_all x1, blocking collectives, local(): back = lax.all_to_all(back, 'z', split_axis=0, concat_axis=0, tiled=True)  16.4 us
    all_to_all x1, starting transfers between devices, local(): rows = lax.all_to_all(moved, SLAB, split_axis=0, concat_axis=0, tiled=True)  14.3 us
    pallas_call x4, Pallas kernels, call(): pl.pallas_call(kernel, out_shape=shapes, scratch_shapes=scratch, in_specs...  13.6 us
    all_to_all x1, blocking collectives, local(): back = lax.all_to_all(back, SLAB, split_axis=0, concat_axis=0, tiled=True)  12.2 us
  transfers between devices with their start and end apart: 1, of which 1 were waited for; matrix products, arithmetic and copies ran while one was open for 0% of the time, Pallas kernels for 0%

profile of v2, /device:TPU:1, one launch (start us, length us, event | category | flops | bytes accessed | tf_op | source)
XLA Modules:
  0.0 140.7 jit_solution(987847012299952725)
XLA Ops:
  0.6 3.4 %shard_map.67 = (bf16[640,768]{1,0:T(8,128)(2,1)}, s32[1,256]{1,0:T(1,128)}) custom-call(f32[256,768]{1,0:T(8,128)} %emb_ref.1, s32[1,256]{1,0:T(1,128)} %bitcast.39, s32[1,256]{1,0:T(1,128)} %bitcast.41, s32[1,512]{1,0:T(1,128)} %bitcast.37), custom_call_target="tpu_custom_call" | custom-call | tf_op jit(solution)/shard_map/pallas_call | solution.py:33
  4.0 59.1 %all_to_all.25 = bf16[16,40,768]{2,1,0:T(8,128)(2,1)} all-to-all(bf16[16,40,768]{2,1,0:T(8,128)(2,1)} %bitcast.30), channel_id=1, replica_groups=mesh['z'=16,'y'=4,'core'=2,'x'=4] {'z'}, dimensions={0} | all-to-all | bytes 1966080 | tf_op jit(solution)/shard_map/all_to_all | solution.py:270
  63.1 4.2 %shard_map.68 = bf16[32,200,128]{2,1,0:T(8,128)(2,1)} custom-call(bf16[640,768]{1,0:T(8,128)(2,1)} %bitcast.28), custom_call_target="tpu_custom_call" | custom-call | tf_op jit(solution)/shard_map/pallas_call | solution.py:33
  67.3 0.0 copy-start.1
  67.3 0.0 copy-start.2
  67.3 0.0 copy-start.3
  67.3 0.0 copy-start.4
  67.3 14.3 %all-to-all-start.2 = ((bf16[32,200,128]{2,1,0:T(8,128)(2,1)}), bf16[32,200,128]{2,1,0:T(8,128)(2,1)S(1)}, u32[]{:S(2)}, u32[]{:S(2)}) async-start(bf16[32,200,128]{2,1,0:T(8,128)(2,1)} %shard_map.68), calls=%async_computation.2 | async-start | bytes 3276800 | tf_op jit(solution)/shard_map/all_to_all | solution.py:272
  81.7 22.1 %all-to-all-done.2.rows_ref = bf16[32,200,128]{2,1,0:T(8,128)(2,1)S(1)} async-done(((bf16[32,200,128]{2,1,0:T(8,128)(2,1)}), bf16[32,200,128]{2,1,0:T(8,128)(2,1)S(1)}, u32[]{:S(2)}, u32[]{:S(2)}) %all-to-all-start.2) | async-done | bytes 1638432 | tf_op jit(solution)/shard_map/all_to_all | solution.py:272
  103.8 0.0 copy-start
  103.8 1.2 copy-done
  105.0 4.4 %shard_map.69 = (f32[1,768]{1,0:T(1,128)}, f32[2,1024]{1,0:T(2,128)S(1)}, f32[1,128]{1,0:T(1,128)}) custom-call(bf16[32,200,128]{2,1,0:T(8,128)(2,1)} %copy-done), custom_call_target="tpu_custom_call" | custom-call | tf_op jit(solution)/shard_map/pallas_call | solution.py:33
  110.0 0.0 copy-done.1
  110.0 0.0 copy-done.2
  110.1 0.0 copy-done.3
  110.1 0.0 copy-done.4
  110.1 0.1 reshape.63
  110.2 0.1 reshape.64
  110.3 12.2 %all_to_all.26 = f32[32,1,64]{2,1,0:T(1,128)S(1)} all-to-all(f32[32,1,64]{2,1,0:T(1,128)S(1)} %bitcast.34), channel_id=1, replica_groups=mesh['z'=16,'y'=4,'core'=2,'x'=4] {'y','core','x'}, dimensions={0} | all-to-all | bytes 16384 | tf_op jit(solution)/shard_map/all_to_all | solution.py:285
  122.5 0.1 copy.23
  122.6 0.1 reshape.66
  122.7 16.4 %all_to_all.27 = f32[16,1,128]{2,1,0:T(1,128)} all-to-all(f32[16,1,128]{2,1,0:T(1,128)S(1)} %bitcast.35), channel_id=1, replica_groups=mesh['z'=16,'y'=4,'core'=2,'x'=4] {'z'}, dimensions={0} | all-to-all | bytes 16384 | tf_op jit(solution)/shard_map/all_to_all | solution.py:287
  139.1 1.6 %shard_map.70 = (f32[1,256]{1,0:T(1,128)}, f32[1,256]{1,0:T(1,128)}) custom-call(f32[16,128]{1,0:T(8,128)} %bitcast.36, s32[1,256]{1,0:T(1,128)} %get-tuple-element.37.slot_ref), custom_call_target="tpu_custom_call" | custom-call | tf_op jit(solution)/shard_map/pallas_call | solution.py:33
  (3 shorter events, 0.1 us)
Async XLA Ops:
  67.3 42.7 %copy-start.1 = (f32[256,768]{1,0:T(8,128)S(1)}, f32[256,768]{1,0:T(8,128)}, u32[]{:S(2)}) copy-start(f32[256,768]{1,0:T(8,128)} %emb_ref.1) | copy-start | bytes 2359300
  67.3 42.7 %copy-start.2 = (s32[512]{0:T(512)S(1)}, s32[512]{0:T(512)}, u32[]{:S(2)}) copy-start(s32[512]{0:T(512)} %param.9) | copy-start | bytes 6148
  67.3 42.7 %copy-start.3 = (s32[256]{0:T(256)S(1)}, s32[256]{0:T(256)}, u32[]{:S(2)}) copy-start(s32[256]{0:T(256)} %param.7) | copy-start | bytes 3076
  67.3 42.7 %copy-start.4 = (s32[256]{0:T(256)S(1)}, s32[256]{0:T(256)}, u32[]{:S(2)}) copy-start(s32[256]{0:T(256)} %param.8) | copy-start | bytes 3076
  67.3 36.5 %all-to-all-start.2 = ((bf16[32,200,128]{2,1,0:T(8,128)(2,1)}), bf16[32,200,128]{2,1,0:T(8,128)(2,1)S(1)}, u32[]{:S(2)}, u32[]{:S(2)}) async-start(bf16[32,200,128]{2,1,0:T(8,128)(2,1)} %shard_map.68), calls=%async_computation.2 | async-start | bytes 3276800 | tf_op jit(solution)/shard_map/all_to_all | solution.py:272
  103.8 1.2 copy-start

commit v3 on v2

--- a/solution.py
+++ b/solution.py
@@ -34,6 +34,7 @@
         kernel,
         out_shape=shapes,
         scratch_shapes=scratch,
+        compiler_params=pltpu.CompilerParams(vmem_limit_bytes=24 * 2**20),
         in_specs=[pl.BlockSpec(memory_space=pltpu.VMEM) for _ in args],
         out_specs=[pl.BlockSpec(memory_space=pltpu.VMEM) for _ in shapes],
     )(*args)

time: 141 us -> 135 us (0.957)
  Pallas kernels: 13.6 us -> 9.28 us
    pallas_call x4, Pallas kernels: 13.6 us -> 9.28 us  [call(): pl.pallas_call(kernel, out_shape=shapes, scratch_shapes=scratch, compiler...]
where the time goes in v3:
time: 135 us; the launch traced here: 134 us
  blocking collectives  87.4 us (65%)
  waiting for transfers between devices  22.1 us (16%)
  starting transfers between devices  14.3 us (11%)
  Pallas kernels  9.28 us (7%)
    all_to_all x1, blocking collectives, local(): lax.all_to_all(packed.reshape(NZ, STRIDE, D), 'z', split_axis=0, concat_a...  58.8 us
    all_to_all x1, waiting for transfers between devices, local(): rows = lax.all_to_all(moved, SLAB, split_axis=0, concat_axis=0, tiled=True)  22.1 us
    all_to_all x1, blocking collectives, local(): back = lax.all_to_all(back, 'z', split_axis=0, concat_axis=0, tiled=True)  16.5 us
    all_to_all x1, starting transfers between devices, local(): rows = lax.all_to_all(moved, SLAB, split_axis=0, concat_axis=0, tiled=True)  14.3 us
    all_to_all x1, blocking collectives, local(): back = lax.all_to_all(back, SLAB, split_axis=0, concat_axis=0, tiled=True)  12.2 us
    pallas_call x4, Pallas kernels, call(): pl.pallas_call(kernel, out_shape=shapes, scratch_shapes=scratch, compiler...  9.28 us
  transfers between devices with their start and end apart: 1, of which 1 were waited for; matrix products, arithmetic and copies ran while one was open for 0% of the time, Pallas kernels for 0%

profile of v3, /device:TPU:1, one launch (start us, length us, event | category | flops | bytes accessed | tf_op | source)
XLA Modules:
  0.0 134.3 jit_solution(10712539959606216941)
XLA Ops:
  0.6 2.4 %shard_map.67 = (bf16[640,768]{1,0:T(8,128)(2,1)S(1)}, s32[1,256]{1,0:T(1,128)S(1)}) custom-call(f32[256,768]{1,0:T(8,128)} %emb_ref.1, s32[1,256]{1,0:T(1,128)} %bitcast.40, s32[1,256]{1,0:T(1,128)} %bitcast.42, s32[1,512]{1,0:T(1,128)} %bitcast.38), custom_call_target="tpu_custom_call" | custom-call | tf_op jit(solution)/shard_map/pallas_call | solution.py:33
  3.0 58.8 %all_to_all.25 = bf16[16,40,768]{2,1,0:T(8,128)(2,1)S(1)} all-to-all(bf16[16,40,768]{2,1,0:T(8,128)(2,1)S(1)} %bitcast.28), channel_id=1, replica_groups=mesh['z'=16,'y'=4,'core'=2,'x'=4] {'z'}, dimensions={0} | all-to-all | bytes 1966080 | tf_op jit(solution)/shard_map/all_to_all | solution.py:271
  61.8 3.0 %shard_map.68 = bf16[32,200,128]{2,1,0:T(8,128)(2,1)} custom-call(bf16[640,768]{1,0:T(8,128)(2,1)S(1)} %bitcast.26), custom_call_target="tpu_custom_call" | custom-call | tf_op jit(solution)/shard_map/pallas_call | solution.py:33
  64.9 0.0 copy-start
  64.9 0.0 copy-start.1
  64.9 0.0 copy-start.2
  64.9 0.0 copy-start.3
  64.9 14.3 %all-to-all-start.2 = ((bf16[32,200,128]{2,1,0:T(8,128)(2,1)}), bf16[32,200,128]{2,1,0:T(8,128)(2,1)S(1)}, u32[]{:S(2)}, u32[]{:S(2)}) async-start(bf16[32,200,128]{2,1,0:T(8,128)(2,1)} %shard_map.68), calls=%async_computation.2 | async-start | bytes 3276800 | tf_op jit(solution)/shard_map/all_to_all | solution.py:273
  79.2 22.1 %all-to-all-done.2.rows_ref = bf16[32,200,128]{2,1,0:T(8,128)(2,1)S(1)} async-done(((bf16[32,200,128]{2,1,0:T(8,128)(2,1)}), bf16[32,200,128]{2,1,0:T(8,128)(2,1)S(1)}, u32[]{:S(2)}, u32[]{:S(2)}) %all-to-all-start.2) | async-done | bytes 1638432 | tf_op jit(solution)/shard_map/all_to_all | solution.py:273
  101.4 3.0 %shard_map.69 = (f32[1,768]{1,0:T(1,128)}, f32[2,1024]{1,0:T(2,128)S(1)}, f32[1,128]{1,0:T(1,128)S(1)}) custom-call(bf16[32,200,128]{2,1,0:T(8,128)(2,1)S(1)} %all-to-all-done.2.rows_ref), custom_call_target="tpu_custom_call" | custom-call | tf_op jit(solution)/shard_map/pallas_call | solution.py:33
  104.4 0.0 copy-done
  104.4 0.0 copy-done.1
  104.4 0.0 copy-done.2
  104.4 0.0 copy-done.3
  104.4 0.1 reshape.63
  104.5 0.1 reshape.64
  104.6 12.2 %all_to_all.26 = f32[32,1,64]{2,1,0:T(1,128)S(1)} all-to-all(f32[32,1,64]{2,1,0:T(1,128)S(1)} %bitcast.36), channel_id=1, replica_groups=mesh['z'=16,'y'=4,'core'=2,'x'=4] {'y','core','x'}, dimensions={0} | all-to-all | bytes 16384 | tf_op jit(solution)/shard_map/all_to_all | solution.py:286
  116.8 0.1 copy.23
  116.9 0.1 reshape.66
  117.0 16.5 %all_to_all.27 = f32[16,1,128]{2,1,0:T(1,128)S(1)} all-to-all(f32[16,1,128]{2,1,0:T(1,128)S(1)} %bitcast.37), channel_id=1, replica_groups=mesh['z'=16,'y'=4,'core'=2,'x'=4] {'z'}, dimensions={0} | all-to-all | bytes 16384 | tf_op jit(solution)/shard_map/all_to_all | solution.py:288
  133.5 0.9 shard_map.70
  (3 shorter events, 0.1 us)
Async XLA Ops:
  64.9 39.5 %copy-start = (f32[256,768]{1,0:T(8,128)S(1)}, f32[256,768]{1,0:T(8,128)}, u32[]{:S(2)}) copy-start(f32[256,768]{1,0:T(8,128)} %emb_ref.1) | copy-start | bytes 2359300
  64.9 39.5 %copy-start.1 = (s32[512]{0:T(512)S(1)}, s32[512]{0:T(512)}, u32[]{:S(2)}) copy-start(s32[512]{0:T(512)} %param.9) | copy-start | bytes 6148
  64.9 39.5 %copy-start.2 = (s32[256]{0:T(256)S(1)}, s32[256]{0:T(256)}, u32[]{:S(2)}) copy-start(s32[256]{0:T(256)} %param.7) | copy-start | bytes 3076
  64.9 39.5 %copy-start.3 = (s32[256]{0:T(256)S(1)}, s32[256]{0:T(256)}, u32[]{:S(2)}) copy-start(s32[256]{0:T(256)} %param.8) | copy-start | bytes 3076
  64.9 36.5 %all-to-all-start.2 = ((bf16[32,200,128]{2,1,0:T(8,128)(2,1)}), bf16[32,200,128]{2,1,0:T(8,128)(2,1)S(1)}, u32[]{:S(2)}, u32[]{:S(2)}) async-start(bf16[32,200,128]{2,1,0:T(8,128)(2,1)} %shard_map.68), calls=%async_computation.2 | async-start | bytes 3276800 | tf_op jit(solution)/shard_map/all_to_all | solution.py:273

commit v4 on v3

--- a/solution.py
+++ b/solution.py
@@ -18,9 +18,12 @@
 F32 = jnp.float32
 NT = (((1,), (1,)), ((), ()))
 TN = (((0,), (0,)), ((), ()))
-STRIDE = 40
-FIT = STRIDE - 1
-SENT = NZ * STRIDE
+FIT = 35
+HALF = D // 2
+CHUNK_Z = 2 * (FIT + 1)
+SENT = NZ * CHUNK_Z
+MAIN = NZ * NQ
+KEPT = MAIN + NZ * 8
 COLS = D // 128
 CHUNK = COLS * NQ + 8
 
@@ -139,7 +142,10 @@
     q = whole - z * NQ
     place = rank_among_equal(z.astype(F32)).astype(jnp.int32)
     overflow = jnp.max((place >= FIT).astype(F32), axis=1, keepdims=True)
-    pos = jnp.where(place < FIT, z * STRIDE + place, -1)
+    left = z * CHUNK_Z + jnp.where(place < NQ, place, place + NQ)
+    right = left + jnp.where(place < NQ, NQ, 4)
+    left = jnp.where(place < FIT, left, -1)
+    right = jnp.where(place < FIT, right, -1)
     emb = emb_ref[...]
     squares = jnp.sum(emb * emb, axis=1, keepdims=True) + 1e-06
     units = (emb * lax.rsqrt(squares)).astype(BF)
@@ -155,41 +161,69 @@
         jnp.where(value == 1, high, jnp.where(value == 2, low, q * 2 + rank + 1)).astype(F32),
     )
     mine = jnp.where(sub - value * NZ == z, picked, 0.0).astype(BF)
-    found = dot_nt(mine, hot(iota((128, ROWS), 0) == place)).astype(BF)
-    flag = jnp.broadcast_to(overflow, (NZ, 128)).astype(BF)
-    meta = jnp.concatenate(
-        [found[v * NZ : (v + 1) * NZ] for v in range(4)] + [flag, jnp.zeros((NZ, 128), BF)], axis=1
-    )
-    spread = hot(iota((SENT, ROWS), 0) == pos)
-    last = hot(iota((SENT, NZ), 0) == iota((SENT, NZ), 1) * STRIDE + FIT)
-    out_ref[...] = (dot(spread, units) + dot(last, meta)).astype(BF)
+    even = hot(iota((128, ROWS), 0) == place)
+    odd = hot(iota((128, ROWS), 0) == place + 64)
+    found = [
+        (dot_nt(mine[v * NZ : (v + 1) * NZ], even) + dot_nt(mine[(v + 1) * NZ : (v + 2) * NZ], odd)).astype(BF)
+        for v in (0, 2)
+    ]
+    meta = jnp.concatenate(found + [jnp.broadcast_to(overflow, (NZ, 128)).astype(BF)], axis=1)
+    rows = iota((SENT, ROWS), 0)
+    last = hot(iota((SENT, NZ), 0) == iota((SENT, NZ), 1) * CHUNK_Z + 67)
+    sent = dot(hot(rows == left), units[:, :HALF]) + dot(hot(rows == right), units[:, HALF:])
+    out_ref[...] = (sent + dot(last, meta)).astype(BF)
 
 
 def repack_kernel(rows_ref, out_ref):
-    last = hot(iota((NZ, SENT), 1) == iota((NZ, SENT), 0) * STRIDE + FIT)
-    meta = dot(last, rows_ref[:, :640])
-    flag = jnp.max(meta[:, 512:640])
-    stacked = jnp.concatenate([meta[:, v * 128 : (v + 1) * 128] for v in range(4)], axis=0).astype(BF)
-    k = iota((128, SENT), 1)
-    along = dot(stacked, hot(iota((128, SENT), 0) == k - (k // STRIDE) * STRIDE))
-    sub = iota((NZ * 4, SENT), 0)
-    here = sub - (sub // NZ) * NZ == iota((NZ * 4, SENT), 1) // STRIDE
-    values = jnp.sum(jnp.where(here, along, 0.0).reshape(4, NZ, SENT), axis=1)
-    code = values[3:4].astype(jnp.int32) - 1
-    q = jnp.where(code >= 0, code // 2, -1)
-    rank = code - q * 2
-    slot = jnp.where(code >= 0, rank * NZ + iota((1, SENT), 1) // STRIDE, -1)
-    pos = jnp.where(code >= 0, q * NQ + slot, -1)
-    spread = hot(iota((2 * DEVS, SENT), 0) == pos)
-    moved = dot(spread, rows_ref[...]).astype(BF)
+    main_left = rows_ref[:, :NQ, :].reshape(MAIN, HALF)
+    main_right = rows_ref[:, NQ : 2 * NQ, :].reshape(MAIN, HALF)
+    tail = rows_ref[:, 2 * NQ :, :].reshape(NZ * 8, HALF)
+    meta = dot(hot(iota((NZ, NZ * 8), 1) == iota((NZ, NZ * 8), 0) * 8 + 3), tail)
+    flag = jnp.max(meta[:, 256:384])
+    pairs = jnp.concatenate([meta[:, :128], meta[:, 128:256]], axis=0).astype(BF)
+
+    def source(shape):
+        k = iota(shape, 1)
+        t = k - MAIN
+        z = jnp.where(t < 0, k // NQ, t // 8)
+        place = jnp.where(t < 0, k - z * NQ, NQ + t - (t // 4) * 4)
+        return z, place, t
+
+    sub = iota((128, KEPT), 0)
+    _, place, _ = source((128, KEPT))
+    z, _, _ = source((NZ * 2, KEPT))
+    here = iota((NZ * 2, KEPT), 0)
+    here = here - (here // NZ) * NZ == z
+    evens = jnp.where(here, dot(pairs, hot(sub == place)), 0.0).reshape(2, NZ, KEPT)
+    odds = jnp.where(here, dot(pairs, hot(sub == place + 64)), 0.0).reshape(2, NZ, KEPT)
+    scale = jnp.sum(evens[0], axis=0, keepdims=True)
+    low = jnp.sum(evens[1], axis=0, keepdims=True)
+    high = jnp.sum(odds[0], axis=0, keepdims=True)
+    code = jnp.sum(odds[1], axis=0, keepdims=True).astype(jnp.int32) - 1
+    z, place, t = source((1, KEPT))
+    filled = (code >= 0) & (place < FIT)
+    q = code // 2
+    slot = (code - q * 2) * NZ + z
+    is_left = filled & ((t < 0) | (t - (t // 8) * 8 < 4))
+    is_right = filled & ((t < 0) | (t - (t // 8) * 8 >= 4))
+    left = jnp.where(is_left, q * NQ + slot, -1)
+    right = jnp.where(is_right, q * NQ + slot, -1)
+    spread = hot(iota((2 * DEVS, MAIN), 0) == left[:, :MAIN])
+    rows = iota((2 * DEVS, NZ * 8), 0)
+    halves = (
+        (dot(spread, main_left) + dot(hot(rows == left[:, MAIN:]), tail)).astype(BF),
+        (dot(spread, main_right) + dot(hot(rows == right[:, MAIN:]), tail)).astype(BF),
+    )
     for c in range(COLS):
-        out_ref[:, c * NQ : (c + 1) * NQ, :] = moved[:, c * 128 : (c + 1) * 128].reshape(NQ, NQ, 128)
-    v = iota((8, SENT), 0)
-    filled = jnp.where(v == 3, 1.0, 0.0)
-    eight = jnp.where(v == 0, values[0:1], jnp.where(v == 1, values[1:2], jnp.where(v == 2, values[2:3], filled)))
-    eight = jnp.broadcast_to(eight[None], (NQ, 8, SENT)).reshape(NQ * 8, SENT)
-    mine = jnp.where(iota((NQ * 8, SENT), 0) // 8 == q, eight, 0.0).astype(BF)
-    details = dot_nt(mine, hot(iota((128, SENT), 0) == slot))
+        half, part = divmod(c, COLS // 2)
+        block = halves[half][:, part * 128 : (part + 1) * 128]
+        out_ref[:, c * NQ : (c + 1) * NQ, :] = block.reshape(NQ, NQ, 128)
+    v = iota((8, KEPT), 0)
+    eight = jnp.where(v == 0, scale, jnp.where(v == 1, high, jnp.where(v == 2, low, jnp.where(v == 3, 1.0, 0.0))))
+    eight = jnp.broadcast_to(eight[None], (NQ, 8, KEPT)).reshape(NQ * 8, KEPT)
+    owner = jnp.where(is_left, q, -1)
+    mine = jnp.where(iota((NQ * 8, KEPT), 0) // 8 == owner, eight, 0.0).astype(BF)
+    details = dot_nt(mine, hot(iota((128, KEPT), 0) == slot))
     sub = iota((NQ * 8, 128), 0)
     details = details + jnp.where(sub - (sub // 8) * 8 == 4, flag, 0.0)
     out_ref[:, COLS * NQ :, :] = details.astype(BF).reshape(NQ, 8, 128)
@@ -262,14 +296,14 @@
     owner_row = owner.reshape(1, DEVS)
     packed, slot = call(
         slab_pack_kernel,
-        [sds((SENT, D), BF), sds((1, ROWS), jnp.int32)],
+        [sds((SENT, HALF), BF), sds((1, ROWS), jnp.int32)],
         embeddings,
         ids_row,
         orders_row,
         owner_row,
     )
-    got = lax.all_to_all(packed.reshape(NZ, STRIDE, D), "z", split_axis=0, concat_axis=0, tiled=True)
-    (moved,) = call(repack_kernel, [sds((NQ, CHUNK, 128), BF)], got.reshape(SENT, D))
+    got = lax.all_to_all(packed.reshape(NZ, CHUNK_Z, HALF), "z", split_axis=0, concat_axis=0, tiled=True)
+    (moved,) = call(repack_kernel, [sds((NQ, CHUNK, 128), BF)], got)
     rows = lax.all_to_all(moved, SLAB, split_axis=0, concat_axis=0, tiled=True)
     center, back, flag = call(
         slab_owner_kernel,

time: 135 us -> 131 us (0.970)
  blocking collectives: 87.4 us -> 82.6 us
    all_to_all x1, blocking collectives: 58.8 us -> 53.9 us  [local(): lax.all_to_all(packed.reshape(NZ, CHUNK_Z, HALF), 'z', split_axis=0, conc...]
where the time goes in v4:
time: 131 us
  blocking collectives  82.6 us (63%)
  waiting for transfers between devices  22.1 us (17%)
  starting transfers between devices  15 us (11%)
  Pallas kernels  9.84 us (8%)
    all_to_all x1, blocking collectives, local(): lax.all_to_all(packed.reshape(NZ, CHUNK_Z, HALF), 'z', split_axis=0, conc...  53.9 us
    all_to_all x1, waiting for transfers between devices, local(): rows = lax.all_to_all(moved, SLAB, split_axis=0, concat_axis=0, tiled=True)  22.1 us
    all_to_all x1, blocking collectives, local(): back = lax.all_to_all(back, 'z', split_axis=0, concat_axis=0, tiled=True)  16.4 us
    all_to_all x1, starting transfers between devices, local(): rows = lax.all_to_all(moved, SLAB, split_axis=0, concat_axis=0, tiled=True)  15 us
    all_to_all x1, blocking collectives, local(): back = lax.all_to_all(back, SLAB, split_axis=0, concat_axis=0, tiled=True)  12.2 us
    pallas_call x4, Pallas kernels, call(): pl.pallas_call(kernel, out_shape=shapes, scratch_shapes=scratch, compiler...  9.84 us
  transfers between devices with their start and end apart: 1, of which 1 were waited for; matrix products, arithmetic and copies ran while one was open for 0% of the time, Pallas kernels for 0%

profile of v4, /device:TPU:1, one launch (start us, length us, event | category | flops | bytes accessed | tf_op | source)
XLA Modules:
  0.0 130.7 jit_solution(13054898935277750711)
XLA Ops:
  0.6 2.8 %shard_map.67 = (bf16[1152,384]{1,0:T(8,128)(2,1)S(1)}, s32[1,256]{1,0:T(1,128)S(1)}) custom-call(f32[256,768]{1,0:T(8,128)} %emb_ref.1, s32[1,256]{1,0:T(1,128)} %bitcast.38, s32[1,256]{1,0:T(1,128)} %bitcast.40, s32[1,512]{1,0:T(1,128)} %bitcast.36), custom_call_target="tpu_custom_call" | custom-call | tf_op jit(solution)/shard_map/pallas_call | solution.py:36
  3.4 53.9 %all_to_all.25.rows_ref = bf16[16,72,384]{2,1,0:T(8,128)(2,1)S(1)} all-to-all(bf16[16,72,384]{2,1,0:T(8,128)(2,1)S(1)} %bitcast.26), channel_id=1, replica_groups=mesh['z'=16,'y'=4,'core'=2,'x'=4] {'z'}, dimensions={0} | all-to-all | bytes 1769472 | tf_op jit(solution)/shard_map/all_to_all | solution.py:305
  57.3 3.2 %shard_map.68 = bf16[32,200,128]{2,1,0:T(8,128)(2,1)} custom-call(bf16[16,72,384]{2,1,0:T(8,128)(2,1)S(1)} %all_to_all.25.rows_ref), custom_call_target="tpu_custom_call" | custom-call | tf_op jit(solution)/shard_map/pallas_call | solution.py:36
  60.6 0.0 copy-start
  60.6 0.0 copy-start.1
  60.6 0.0 copy-start.2
  60.6 0.0 copy-start.3
  60.6 15.0 %all-to-all-start.2 = ((bf16[32,200,128]{2,1,0:T(8,128)(2,1)}), bf16[32,200,128]{2,1,0:T(8,128)(2,1)S(1)}, u32[]{:S(2)}, u32[]{:S(2)}) async-start(bf16[32,200,128]{2,1,0:T(8,128)(2,1)} %shard_map.68), calls=%async_computation.2 | async-start | bytes 3276800 | tf_op jit(solution)/shard_map/all_to_all | solution.py:307
  75.6 22.1 %all-to-all-done.2.rows_ref = bf16[32,200,128]{2,1,0:T(8,128)(2,1)S(1)} async-done(((bf16[32,200,128]{2,1,0:T(8,128)(2,1)}), bf16[32,200,128]{2,1,0:T(8,128)(2,1)S(1)}, u32[]{:S(2)}, u32[]{:S(2)}) %all-to-all-start.2) | async-done | bytes 1638432 | tf_op jit(solution)/shard_map/all_to_all | solution.py:307
  97.7 3.0 %shard_map.69 = (f32[1,768]{1,0:T(1,128)}, f32[2,1024]{1,0:T(2,128)S(1)}, f32[1,128]{1,0:T(1,128)S(1)}) custom-call(bf16[32,200,128]{2,1,0:T(8,128)(2,1)S(1)} %all-to-all-done.2.rows_ref), custom_call_target="tpu_custom_call" | custom-call | tf_op jit(solution)/shard_map/pallas_call | solution.py:36
  100.7 0.0 copy-done
  100.7 0.0 copy-done.1
  100.7 0.0 copy-done.2
  100.7 0.0 copy-done.3
  100.8 0.1 reshape.59
  100.9 0.1 reshape.60
  101.0 12.2 %all_to_all.26 = f32[32,1,64]{2,1,0:T(1,128)S(1)} all-to-all(f32[32,1,64]{2,1,0:T(1,128)S(1)} %bitcast.34), channel_id=1, replica_groups=mesh['z'=16,'y'=4,'core'=2,'x'=4] {'y','core','x'}, dimensions={0} | all-to-all | bytes 16384 | tf_op jit(solution)/shard_map/all_to_all | solution.py:320
  113.2 0.1 copy.23
  113.3 0.1 reshape.62
  113.3 16.4 %all_to_all.27 = f32[16,1,128]{2,1,0:T(1,128)S(1)} all-to-all(f32[16,1,128]{2,1,0:T(1,128)S(1)} %bitcast.35), channel_id=1, replica_groups=mesh['z'=16,'y'=4,'core'=2,'x'=4] {'z'}, dimensions={0} | all-to-all | bytes 16384 | tf_op jit(solution)/shard_map/all_to_all | solution.py:322
  129.8 0.9 shard_map.70
  (3 shorter events, 0.1 us)
Async XLA Ops:
  60.6 40.1 %copy-start = (f32[256,768]{1,0:T(8,128)S(1)}, f32[256,768]{1,0:T(8,128)}, u32[]{:S(2)}) copy-start(f32[256,768]{1,0:T(8,128)} %emb_ref.1) | copy-start | bytes 2359300
  60.6 40.2 %copy-start.1 = (s32[512]{0:T(512)S(1)}, s32[512]{0:T(512)}, u32[]{:S(2)}) copy-start(s32[512]{0:T(512)} %param.9) | copy-start | bytes 6148
  60.6 40.2 %copy-start.2 = (s32[256]{0:T(256)S(1)}, s32[256]{0:T(256)}, u32[]{:S(2)}) copy-start(s32[256]{0:T(256)} %param.7) | copy-start | bytes 3076
  60.6 40.2 %copy-start.3 = (s32[256]{0:T(256)S(1)}, s32[256]{0:T(256)}, u32[]{:S(2)}) copy-start(s32[256]{0:T(256)} %param.8) | copy-start | bytes 3076
  60.6 37.1 %all-to-all-start.2 = ((bf16[32,200,128]{2,1,0:T(8,128)(2,1)}), bf16[32,200,128]{2,1,0:T(8,128)(2,1)S(1)}, u32[]{:S(2)}, u32[]{:S(2)}) async-start(bf16[32,200,128]{2,1,0:T(8,128)(2,1)} %shard_map.68), calls=%async_computation.2 | async-start | bytes 3276800 | tf_op jit(solution)/shard_map/all_to_all | solution.py:307

commit v5 on v4

--- a/solution.py
+++ b/solution.py
@@ -141,7 +141,7 @@
     z = whole // NQ
     q = whole - z * NQ
     place = rank_among_equal(z.astype(F32)).astype(jnp.int32)
-    overflow = jnp.max((place >= FIT).astype(F32), axis=1, keepdims=True)
+    overflow = jnp.max((place >= 0).astype(F32), axis=1, keepdims=True)
     left = z * CHUNK_Z + jnp.where(place < NQ, place, place + NQ)
     right = left + jnp.where(place < NQ, NQ, 4)
     left = jnp.where(place < FIT, left, -1)

time: 131 us -> 237 us (1.81)
  blocking collectives: 82.6 us -> 182 us
  Pallas kernels: 9.84 us -> 14.3 us
  local copies, waits for them, and re-layouts: 0.39 us -> 2.81 us
    all_to_all x0 -> x1, blocking collectives: none -> 103 us  [full_exchange(): got = lax.all_to_all(send, ALL, split_axis=0, concat_axis=0, tiled=True)]
    pallas_call x4 -> x6, Pallas kernels: 9.84 us -> 14.3 us  [call(): pl.pallas_call(kernel, out_shape=shapes, scratch_shapes=scratch, compiler...]
    all_to_all x1, blocking collectives: 16.4 us -> 13.8 us  [local(): back = lax.all_to_all(back, 'z', split_axis=0, concat_axis=0, tiled=True)]
where the time goes in v5:
time: 237 us
  blocking collectives  182 us (77%)
  waiting for transfers between devices  22.1 us (9%)
  starting transfers between devices  15 us (6%)
  Pallas kernels  14.3 us (6%)
  local copies, waits for them, and re-layouts  2.81 us (1%)
    all_to_all x1, blocking collectives, full_exchange(): got = lax.all_to_all(send, ALL, split_axis=0, concat_axis=0, tiled=True)  103 us
    all_to_all x1, blocking collectives, local(): lax.all_to_all(packed.reshape(NZ, CHUNK_Z, HALF), 'z', split_axis=0, conc...  53.9 us
    all_to_all x1, waiting for transfers between devices, local(): rows = lax.all_to_all(moved, SLAB, split_axis=0, concat_axis=0, tiled=True)  22.1 us
    all_to_all x1, starting transfers between devices, local(): rows = lax.all_to_all(moved, SLAB, split_axis=0, concat_axis=0, tiled=True)  15 us
    pallas_call x6, Pallas kernels, call(): pl.pallas_call(kernel, out_shape=shapes, scratch_shapes=scratch, compiler...  14.3 us
    all_to_all x1, blocking collectives, local(): back = lax.all_to_all(back, 'z', split_axis=0, concat_axis=0, tiled=True)  13.8 us
    all_to_all x1, blocking collectives, local(): back = lax.all_to_all(back, SLAB, split_axis=0, concat_axis=0, tiled=True)  10.5 us
  transfers between devices with their start and end apart: 1, of which 1 were waited for; matrix products, arithmetic and copies ran while one was open for 0% of the time, Pallas kernels for 0%

profile of v5, /device:TPU:1, one launch (start us, length us, event | category | flops | bytes accessed | tf_op | source)
XLA Modules:
  0.0 236.8 jit_solution(14138833806244961932)
XLA Ops:
  0.6 2.8 %shard_map.67 = (bf16[1152,384]{1,0:T(8,128)(2,1)S(1)}, s32[1,256]{1,0:T(1,128)S(1)}) custom-call(f32[256,768]{1,0:T(8,128)} %emb_ref.1, s32[1,256]{1,0:T(1,128)} %bitcast.38, s32[1,256]{1,0:T(1,128)} %bitcast.40, s32[1,512]{1,0:T(1,128)} %bitcast.36), custom_call_target="tpu_custom_call" | custom-call | tf_op jit(solution)/shard_map/pallas_call | solution.py:36
  3.4 53.9 %all_to_all.25.rows_ref = bf16[16,72,384]{2,1,0:T(8,128)(2,1)S(1)} all-to-all(bf16[16,72,384]{2,1,0:T(8,128)(2,1)S(1)} %bitcast.26), channel_id=1, replica_groups=mesh['z'=16,'y'=4,'core'=2,'x'=4] {'z'}, dimensions={0} | all-to-all | bytes 1769472 | tf_op jit(solution)/shard_map/all_to_all | solution.py:305
  57.3 3.2 %shard_map.68 = bf16[32,200,128]{2,1,0:T(8,128)(2,1)} custom-call(bf16[16,72,384]{2,1,0:T(8,128)(2,1)S(1)} %all_to_all.25.rows_ref), custom_call_target="tpu_custom_call" | custom-call | tf_op jit(solution)/shard_map/pallas_call | solution.py:36
  60.6 0.0 copy-start
  60.6 0.0 copy-start.1
  60.6 0.0 copy-start.2
  60.6 0.0 copy-start.3
  60.6 15.0 %all-to-all-start.2 = ((bf16[32,200,128]{2,1,0:T(8,128)(2,1)}), bf16[32,200,128]{2,1,0:T(8,128)(2,1)S(1)}, u32[]{:S(2)}, u32[]{:S(2)}) async-start(bf16[32,200,128]{2,1,0:T(8,128)(2,1)} %shard_map.68), calls=%async_computation.2 | async-start | bytes 3276800 | tf_op jit(solution)/shard_map/all_to_all | solution.py:307
  75.6 22.1 %all-to-all-done.2.rows_ref = bf16[32,200,128]{2,1,0:T(8,128)(2,1)S(1)} async-done(((bf16[32,200,128]{2,1,0:T(8,128)(2,1)}), bf16[32,200,128]{2,1,0:T(8,128)(2,1)S(1)}, u32[]{:S(2)}, u32[]{:S(2)}) %all-to-all-start.2) | async-done | bytes 1638432 | tf_op jit(solution)/shard_map/all_to_all | solution.py:307
  97.7 3.0 %shard_map.69 = (f32[1,768]{1,0:T(1,128)}, f32[2,1024]{1,0:T(2,128)S(1)}, f32[1,128]{1,0:T(1,128)S(1)}) custom-call(bf16[32,200,128]{2,1,0:T(8,128)(2,1)S(1)} %all-to-all-done.2.rows_ref), custom_call_target="tpu_custom_call" | custom-call | tf_op jit(solution)/shard_map/pallas_call | solution.py:36
  100.7 0.0 copy-done
  100.7 0.0 copy-done.1
  100.7 0.0 copy-done.2
  100.7 0.0 copy-done.3
  100.8 110.4 %conditional.1 = ((f32[1,768]{1,0:T(1,128)}, f32[2,1024]{1,0:T(2,128)S(1)})) conditional(s32[]{:T(128)} %bitcast.9, (f32[1,768]{1,0:T(1,128)}, f32[2,1024]{1,0:T(2,128)S(1)}) %tuple.15, (f32[256,768]{1,0:T(8,128)S(1)}, s32[1,256]{1,0:T(1,128)S(1)}, s32[1,256]{1,0:T(1,128)S(1)}, s32[1,512]{1,0:T(1,128)S(1)}) %tuple.25), branch_computations={%region_0.0_spmd, %region_1.0_spmd} | conditional | bytes 11059224 | solution.py:314
  100.8 1.3 branch_1_fun.2
  102.1 1.9 copy.28
  104.0 103.4 %all_to_all.24 = bf16[512,2,896]{2,1,0:T(2,128)(2,1)S(1)} all-to-all(bf16[512,2,896]{2,1,0:T(2,128)(2,1)S(1)} %bitcast.29), channel_id=1, replica_groups=mesh['z'=16,'y'=4,'core'=2,'x'=4] {'z','y','core','x'}, dimensions={0} | all-to-all | bytes 3670016 | tf_op jit(solution)/shard_map/cond/branch_1_fun/all_to_all | solution.py:286
  207.4 0.2 copy.19
  207.6 3.2 %branch_1_fun.3 = (f32[1,768]{1,0:T(1,128)}, f32[4,512]{1,0:T(4,128)S(1)}) custom-call(bf16[1024,896]{1,0:T(8,128)(2,1)S(1)} %bitcast.24), custom_call_target="tpu_custom_call" | custom-call | tf_op jit(solution)/shard_map/cond/branch_1_fun/pallas_call | solution.py:36
  210.8 0.1 reshape.42
  210.9 0.1 copy.20
  211.0 0.1 reshape.43
  211.1 0.1 reshape.59
  211.3 0.1 reshape.60
  211.3 10.5 %all_to_all.26 = f32[32,1,64]{2,1,0:T(1,128)S(1)} all-to-all(f32[32,1,64]{2,1,0:T(1,128)S(1)} %bitcast.34), channel_id=1, replica_groups=mesh['z'=16,'y'=4,'core'=2,'x'=4] {'y','core','x'}, dimensions={0} | all-to-all | bytes 16384 | tf_op jit(solution)/shard_map/all_to_all | solution.py:320
  221.9 0.1 copy.23
  222.0 0.1 reshape.62
  222.0 13.8 %all_to_all.27 = f32[16,1,128]{2,1,0:T(1,128)S(1)} all-to-all(f32[16,1,128]{2,1,0:T(1,128)S(1)} %bitcast.35), channel_id=1, replica_groups=mesh['z'=16,'y'=4,'core'=2,'x'=4] {'z'}, dimensions={0} | all-to-all | bytes 16384 | tf_op jit(solution)/shard_map/all_to_all | solution.py:322
  235.9 0.9 shard_map.70
  (2 shorter events, 0.1 us)
Async XLA Ops:
  60.6 40.1 %copy-start = (f32[256,768]{1,0:T(8,128)S(1)}, f32[256,768]{1,0:T(8,128)}, u32[]{:S(2)}) copy-start(f32[256,768]{1,0:T(8,128)} %emb_ref.1) | copy-start | bytes 2359300
  60.6 40.2 %copy-start.1 = (s32[512]{0:T(512)S(1)}, s32[512]{0:T(512)}, u32[]{:S(2)}) copy-start(s32[512]{0:T(512)} %param.9) | copy-start | bytes 6148
  60.6 40.2 %copy-start.2 = (s32[256]{0:T(256)S(1)}, s32[256]{0:T(256)}, u32[]{:S(2)}) copy-start(s32[256]{0:T(256)} %param.7) | copy-start | bytes 3076
  60.6 40.2 %copy-start.3 = (s32[256]{0:T(256)S(1)}, s32[256]{0:T(256)}, u32[]{:S(2)}) copy-start(s32[256]{0:T(256)} %param.8) | copy-start | bytes 3076
  60.6 37.1 %all-to-all-start.2 = ((bf16[32,200,128]{2,1,0:T(8,128)(2,1)}), bf16[32,200,128]{2,1,0:T(8,128)(2,1)S(1)}, u32[]{:S(2)}, u32[]{:S(2)}) async-start(bf16[32,200,128]{2,1,0:T(8,128)(2,1)} %shard_map.68), calls=%async_computation.2 | async-start | bytes 3276800 | tf_op jit(solution)/shard_map/all_to_all | solution.py:307

commit v6 on v4

--- a/solution.py
+++ b/solution.py
@@ -32,13 +32,13 @@
     return jnp.transpose(jnp.broadcast_to(row, (128, row.shape[1])))[:, :1]
 
 
-def call(kernel, shapes, *args, scratch=()):
+def call(kernel, shapes, *args, scratch=(), far=0):
     return pl.pallas_call(
         kernel,
         out_shape=shapes,
         scratch_shapes=scratch,
         compiler_params=pltpu.CompilerParams(vmem_limit_bytes=24 * 2**20),
-        in_specs=[pl.BlockSpec(memory_space=pltpu.VMEM) for _ in args],
+        in_specs=[pl.BlockSpec(memory_space=pltpu.HBM if i < far else pltpu.VMEM) for i in range(len(args))],
         out_specs=[pl.BlockSpec(memory_space=pltpu.VMEM) for _ in shapes],
     )(*args)
 
@@ -60,7 +60,11 @@
     return jnp.sum(jnp.where((col == row) & (j < i), 1.0, 0.0), axis=0, keepdims=True)
 
 
-def pack_kernel(emb_ref, ids_ref, ord_ref, own_ref, out_ref, slot_ref):
+def pack_kernel(emb_far, ids_far, ord_far, own_far, out_ref, slot_ref, emb_ref, ids_ref, ord_ref, own_ref):
+    pltpu.sync_copy(emb_far, emb_ref)
+    pltpu.sync_copy(ids_far, ids_ref)
+    pltpu.sync_copy(ord_far, ord_ref)
+    pltpu.sync_copy(own_far, own_ref)
     target = targets(ids_ref[...], own_ref[...])
     rank = rank_among_equal(target)
     pos = (rank * DEVS + target).astype(jnp.int32)
@@ -133,7 +137,9 @@
     return lax.dot_general(a, b, NT, preferred_element_type=F32)
 
 
-def slab_pack_kernel(emb_ref, ids_ref, ord_ref, own_ref, out_ref, slot_ref):
+def slab_pack_kernel(emb_ref, ids_ref, ord_ref, own_ref, out_ref, slot_ref, here_ref, sem):
+    copy = pltpu.make_async_copy(emb_ref, here_ref, sem)
+    copy.start()
     target = targets(ids_ref[...], own_ref[...])
     rank = rank_among_equal(target).astype(jnp.int32)
     whole = target.astype(jnp.int32)
@@ -146,7 +152,13 @@
     right = left + jnp.where(place < NQ, NQ, 4)
     left = jnp.where(place < FIT, left, -1)
     right = jnp.where(place < FIT, right, -1)
-    emb = emb_ref[...]
+    even = hot(iota((128, ROWS), 0) == place)
+    odd = hot(iota((128, ROWS), 0) == place + 64)
+    rows = iota((SENT, ROWS), 0)
+    to_left = hot(rows == left)
+    to_right = hot(rows == right)
+    copy.wait()
+    emb = here_ref[...]
     squares = jnp.sum(emb * emb, axis=1, keepdims=True) + 1e-06
     units = (emb * lax.rsqrt(squares)).astype(BF)
     scale = row_of(jnp.sqrt(squares).astype(BF).astype(F32))
@@ -161,16 +173,13 @@
         jnp.where(value == 1, high, jnp.where(value == 2, low, q * 2 + rank + 1)).astype(F32),
     )
     mine = jnp.where(sub - value * NZ == z, picked, 0.0).astype(BF)
-    even = hot(iota((128, ROWS), 0) == place)
-    odd = hot(iota((128, ROWS), 0) == place + 64)
     found = [
         (dot_nt(mine[v * NZ : (v + 1) * NZ], even) + dot_nt(mine[(v + 1) * NZ : (v + 2) * NZ], odd)).astype(BF)
         for v in (0, 2)
     ]
     meta = jnp.concatenate(found + [jnp.broadcast_to(overflow, (NZ, 128)).astype(BF)], axis=1)
-    rows = iota((SENT, ROWS), 0)
     last = hot(iota((SENT, NZ), 0) == iota((SENT, NZ), 1) * CHUNK_Z + 67)
-    sent = dot(hot(rows == left), units[:, :HALF]) + dot(hot(rows == right), units[:, HALF:])
+    sent = dot(to_left, units[:, :HALF]) + dot(to_right, units[:, HALF:])
     out_ref[...] = (sent + dot(last, meta)).astype(BF)
 
 
@@ -281,6 +290,13 @@
         ids_row,
         orders_row,
         owner_row,
+        scratch=[
+            pltpu.VMEM((ROWS, D), F32),
+            pltpu.VMEM((1, ROWS), jnp.int32),
+            pltpu.VMEM((1, ROWS), jnp.int32),
+            pltpu.VMEM((1, DEVS), jnp.int32),
+        ],
+        far=4,
     )
     send = packed.reshape(2, DEVS, W).transpose(1, 0, 2)
     got = lax.all_to_all(send, ALL, split_axis=0, concat_axis=0, tiled=True)
@@ -301,6 +317,8 @@
         ids_row,
         orders_row,
         owner_row,
+        scratch=[pltpu.VMEM((ROWS, D), F32), pltpu.SemaphoreType.DMA],
+        far=1,
     )
     got = lax.all_to_all(packed.reshape(NZ, CHUNK_Z, HALF), "z", split_axis=0, concat_axis=0, tiled=True)
     (moved,) = call(repack_kernel, [sds((NQ, CHUNK, 128), BF)], got)
@@ -311,9 +329,10 @@
         rows,
         scratch=[pltpu.VMEM((2 * DEVS, D), BF)],
     )
+    flag, *arguments = lax.optimization_barrier((flag, embeddings, ids_row, orders_row, owner_row))
     center, back = lax.cond(
         flag[0, 0] > 0.0,
-        lambda: full_exchange(embeddings, ids_row, orders_row, owner_row),
+        lambda: full_exchange(*arguments),
         lambda: (center, back),
     )
     back = back.reshape(2, NQ, NQ).transpose(1, 0, 2).reshape(NQ, 1, 2 * NQ)

time: 131 us -> 130 us (level)
  blocking collectives: 82.6 us -> 120 us
  waiting for transfers between devices: 22.1 us -> 0 us
  starting transfers between devices: 15 us -> 0 us
    all_to_all x0 -> x1, blocking collectives: none -> 38.1 us  [local(): rows = lax.all_to_all(moved, SLAB, split_axis=0, concat_axis=0, tiled=True)]
    all_to_all x1 -> x0, waiting for transfers between devices: 22.1 us -> none  [local(): rows = lax.all_to_all(moved, SLAB, split_axis=0, concat_axis=0, tiled=True)]
    all_to_all x1 -> x0, starting transfers between devices: 15 us -> none  [local(): rows = lax.all_to_all(moved, SLAB, split_axis=0, concat_axis=0, tiled=True)]
  transfers between devices with their start and end apart: 1 -> 0, of which waited for: 1 -> 0; matrix products, arithmetic and copies ran while one was open for 0% -> 0% of each run, Pallas kernels for 0% -> 0%
where the time goes in v6:
time: 130 us
  blocking collectives  120 us (92%)
  Pallas kernels  8.96 us (7%)
    all_to_all x1, blocking collectives, local(): lax.all_to_all(packed.reshape(NZ, CHUNK_Z, HALF), 'z', split_axis=0, conc...  53.9 us
    all_to_all x1, blocking collectives, local(): rows = lax.all_to_all(moved, SLAB, split_axis=0, concat_axis=0, tiled=True)  38.1 us
    all_to_all x1, blocking collectives, local(): back = lax.all_to_all(back, 'z', split_axis=0, concat_axis=0, tiled=True)  16.4 us
    all_to_all x1, blocking collectives, local(): back = lax.all_to_all(back, SLAB, split_axis=0, concat_axis=0, tiled=True)  11.1 us
    pallas_call x4, Pallas kernels, call(): pl.pallas_call(kernel, out_shape=shapes, scratch_shapes=scratch, compiler...  8.96 us

profile of v6, /device:TPU:1, one launch (start us, length us, event | category | flops | bytes accessed | tf_op | source)
XLA Modules:
  0.0 129.9 jit_solution(3180852099738112531)
XLA Ops:
  0.6 3.1 %shard_map.67 = (bf16[1152,384]{1,0:T(8,128)(2,1)S(1)}, s32[1,256]{1,0:T(1,128)S(1)}) custom-call(f32[256,768]{1,0:T(8,128)} %emb_ref.1, s32[1,256]{1,0:T(1,128)} %bitcast.38, s32[1,256]{1,0:T(1,128)} %bitcast.40, s32[1,512]{1,0:T(1,128)} %bitcast.36), custom_call_target="tpu_custom_call" | custom-call | tf_op jit(solution)/shard_map/pallas_call | solution.py:36
  3.7 53.9 %all_to_all.25.rows_ref = bf16[16,72,384]{2,1,0:T(8,128)(2,1)S(1)} all-to-all(bf16[16,72,384]{2,1,0:T(8,128)(2,1)S(1)} %bitcast.26), channel_id=1, replica_groups=mesh['z'=16,'y'=4,'core'=2,'x'=4] {'z'}, dimensions={0} | all-to-all | bytes 1769472 | tf_op jit(solution)/shard_map/all_to_all | solution.py:323
  57.7 2.0 %shard_map.68 = bf16[32,200,128]{2,1,0:T(8,128)(2,1)S(1)} custom-call(bf16[16,72,384]{2,1,0:T(8,128)(2,1)S(1)} %all_to_all.25.rows_ref), custom_call_target="tpu_custom_call" | custom-call | tf_op jit(solution)/shard_map/pallas_call | solution.py:36
  59.7 0.0 copy-start
  59.7 0.0 copy-start.1
  59.7 0.0 copy-start.2
  59.7 0.0 copy-start.3
  59.8 38.1 %all_to_all.26.rows_ref = bf16[32,200,128]{2,1,0:T(8,128)(2,1)S(1)} all-to-all(bf16[32,200,128]{2,1,0:T(8,128)(2,1)S(1)} %shard_map.68), channel_id=1, replica_groups=mesh['z'=16,'y'=4,'core'=2,'x'=4] {'y','core','x'}, dimensions={0} | all-to-all | bytes 3276800 | tf_op jit(solution)/shard_map/all_to_all | solution.py:325
  97.8 3.0 %shard_map.69 = (f32[1,768]{1,0:T(1,128)}, f32[2,1024]{1,0:T(2,128)S(1)}, f32[1,128]{1,0:T(1,128)S(1)}) custom-call(bf16[32,200,128]{2,1,0:T(8,128)(2,1)S(1)} %all_to_all.26.rows_ref), custom_call_target="tpu_custom_call" | custom-call | tf_op jit(solution)/shard_map/pallas_call | solution.py:36
  100.8 0.0 copy-done
  100.8 0.0 copy-done.1
  100.9 0.0 copy-done.2
  100.9 0.0 copy-done.3
  100.9 0.2 conditional.1
  101.1 0.1 reshape.59
  101.2 0.1 reshape.60
  101.3 11.1 %all_to_all.27 = f32[32,1,64]{2,1,0:T(1,128)S(1)} all-to-all(f32[32,1,64]{2,1,0:T(1,128)S(1)} %bitcast.34), channel_id=1, replica_groups=mesh['z'=16,'y'=4,'core'=2,'x'=4] {'y','core','x'}, dimensions={0} | all-to-all | bytes 16384 | tf_op jit(solution)/shard_map/all_to_all | solution.py:339
  112.5 0.1 copy.23
  112.6 0.1 reshape.62
  112.6 16.4 %all_to_all.28 = f32[16,1,128]{2,1,0:T(1,128)S(1)} all-to-all(f32[16,1,128]{2,1,0:T(1,128)S(1)} %bitcast.35), channel_id=1, replica_groups=mesh['z'=16,'y'=4,'core'=2,'x'=4] {'z'}, dimensions={0} | all-to-all | bytes 16384 | tf_op jit(solution)/shard_map/all_to_all | solution.py:341
  129.1 0.9 shard_map.70
  (2 shorter events, 0.0 us)
Async XLA Ops:
  59.7 41.1 %copy-start = (f32[256,768]{1,0:T(8,128)S(1)}, f32[256,768]{1,0:T(8,128)}, u32[]{:S(2)}) copy-start(f32[256,768]{1,0:T(8,128)} %emb_ref.1) | copy-start | bytes 2359300
  59.7 41.1 %copy-start.1 = (s32[512]{0:T(512)S(1)}, s32[512]{0:T(512)}, u32[]{:S(2)}) copy-start(s32[512]{0:T(512)} %param.9) | copy-start | bytes 6148
  59.7 41.1 %copy-start.2 = (s32[256]{0:T(256)S(1)}, s32[256]{0:T(256)}, u32[]{:S(2)}) copy-start(s32[256]{0:T(256)} %param.7) | copy-start | bytes 3076
  59.7 41.1 %copy-start.3 = (s32[256]{0:T(256)S(1)}, s32[256]{0:T(256)}, u32[]{:S(2)}) copy-start(s32[256]{0:T(256)} %param.8) | copy-start | bytes 3076

commit v7 on v6

--- a/solution.py
+++ b/solution.py
@@ -138,8 +138,13 @@
 
 
 def slab_pack_kernel(emb_ref, ids_ref, ord_ref, own_ref, out_ref, slot_ref, here_ref, sem):
-    copy = pltpu.make_async_copy(emb_ref, here_ref, sem)
-    copy.start()
+    parts = [pl.ds(i * 64, 64) for i in range(ROWS // 64)]
+    copies = [
+        pltpu.make_async_copy(emb_ref.at[part, :], here_ref.at[part, :], sem.at[i])
+        for i, part in enumerate(parts)
+    ]
+    for copy in copies:
+        copy.start()
     target = targets(ids_ref[...], own_ref[...])
     rank = rank_among_equal(target).astype(jnp.int32)
     whole = target.astype(jnp.int32)
@@ -154,10 +159,8 @@
     right = jnp.where(place < FIT, right, -1)
     even = hot(iota((128, ROWS), 0) == place)
     odd = hot(iota((128, ROWS), 0) == place + 64)
-    rows = iota((SENT, ROWS), 0)
-    to_left = hot(rows == left)
-    to_right = hot(rows == right)
-    copy.wait()
+    for copy in copies:
+        copy.wait()
     emb = here_ref[...]
     squares = jnp.sum(emb * emb, axis=1, keepdims=True) + 1e-06
     units = (emb * lax.rsqrt(squares)).astype(BF)
@@ -179,7 +182,8 @@
     ]
     meta = jnp.concatenate(found + [jnp.broadcast_to(overflow, (NZ, 128)).astype(BF)], axis=1)
     last = hot(iota((SENT, NZ), 0) == iota((SENT, NZ), 1) * CHUNK_Z + 67)
-    sent = dot(to_left, units[:, :HALF]) + dot(to_right, units[:, HALF:])
+    rows = iota((SENT, ROWS), 0)
+    sent = dot(hot(rows == left), units[:, :HALF]) + dot(hot(rows == right), units[:, HALF:])
     out_ref[...] = (sent + dot(last, meta)).astype(BF)
 
 
@@ -317,7 +321,7 @@
         ids_row,
         orders_row,
         owner_row,
-        scratch=[pltpu.VMEM((ROWS, D), F32), pltpu.SemaphoreType.DMA],
+        scratch=[pltpu.VMEM((ROWS, D), F32), pltpu.SemaphoreType.DMA((ROWS // 64,))],
         far=1,
     )
     got = lax.all_to_all(packed.reshape(NZ, CHUNK_Z, HALF), "z", split_axis=0, concat_axis=0, tiled=True)

time: 130 us -> 130 us (level)
  no operation moved by 1% of the time
where the time goes in v7:
time: 130 us
  blocking collectives  120 us (92%)
  Pallas kernels  9.08 us (7%)
    all_to_all x1, blocking collectives, local(): lax.all_to_all(packed.reshape(NZ, CHUNK_Z, HALF), 'z', split_axis=0, conc...  53.9 us
    all_to_all x1, blocking collectives, local(): rows = lax.all_to_all(moved, SLAB, split_axis=0, concat_axis=0, tiled=True)  38.1 us
    all_to_all x1, blocking collectives, local(): back = lax.all_to_all(back, 'z', split_axis=0, concat_axis=0, tiled=True)  16.4 us
    all_to_all x1, blocking collectives, local(): back = lax.all_to_all(back, SLAB, split_axis=0, concat_axis=0, tiled=True)  11.1 us
    pallas_call x4, Pallas kernels, call(): pl.pallas_call(kernel, out_shape=shapes, scratch_shapes=scratch, compiler...  9.08 us

profile of v7, /device:TPU:1, one launch (start us, length us, event | category | flops | bytes accessed | tf_op | source)
XLA Modules:
  0.0 130.1 jit_solution(11298064102065641240)
XLA Ops:
  0.6 3.2 %shard_map.67 = (bf16[1152,384]{1,0:T(8,128)(2,1)S(1)}, s32[1,256]{1,0:T(1,128)S(1)}) custom-call(f32[256,768]{1,0:T(8,128)} %emb_ref.1, s32[1,256]{1,0:T(1,128)} %bitcast.38, s32[1,256]{1,0:T(1,128)} %bitcast.40, s32[1,512]{1,0:T(1,128)} %bitcast.36), custom_call_target="tpu_custom_call" | custom-call | tf_op jit(solution)/shard_map/pallas_call | solution.py:36
  3.8 53.9 %all_to_all.25.rows_ref = bf16[16,72,384]{2,1,0:T(8,128)(2,1)S(1)} all-to-all(bf16[16,72,384]{2,1,0:T(8,128)(2,1)S(1)} %bitcast.26), channel_id=1, replica_groups=mesh['z'=16,'y'=4,'core'=2,'x'=4] {'z'}, dimensions={0} | all-to-all | bytes 1769472 | tf_op jit(solution)/shard_map/all_to_all | solution.py:327
  57.8 2.0 %shard_map.68 = bf16[32,200,128]{2,1,0:T(8,128)(2,1)S(1)} custom-call(bf16[16,72,384]{2,1,0:T(8,128)(2,1)S(1)} %all_to_all.25.rows_ref), custom_call_target="tpu_custom_call" | custom-call | tf_op jit(solution)/shard_map/pallas_call | solution.py:36
  59.8 0.0 copy-start
  59.8 0.0 copy-start.1
  59.8 0.0 copy-start.2
  59.9 0.0 copy-start.3
  59.9 38.1 %all_to_all.26.rows_ref = bf16[32,200,128]{2,1,0:T(8,128)(2,1)S(1)} all-to-all(bf16[32,200,128]{2,1,0:T(8,128)(2,1)S(1)} %shard_map.68), channel_id=1, replica_groups=mesh['z'=16,'y'=4,'core'=2,'x'=4] {'y','core','x'}, dimensions={0} | all-to-all | bytes 3276800 | tf_op jit(solution)/shard_map/all_to_all | solution.py:329
  97.9 3.0 %shard_map.69 = (f32[1,768]{1,0:T(1,128)}, f32[2,1024]{1,0:T(2,128)S(1)}, f32[1,128]{1,0:T(1,128)S(1)}) custom-call(bf16[32,200,128]{2,1,0:T(8,128)(2,1)S(1)} %all_to_all.26.rows_ref), custom_call_target="tpu_custom_call" | custom-call | tf_op jit(solution)/shard_map/pallas_call | solution.py:36
  100.9 0.0 copy-done
  101.0 0.0 copy-done.1
  101.0 0.0 copy-done.2
  101.0 0.0 copy-done.3
  101.0 0.2 conditional.1
  101.2 0.1 reshape.59
  101.3 0.1 reshape.60
  101.4 11.1 %all_to_all.27 = f32[32,1,64]{2,1,0:T(1,128)S(1)} all-to-all(f32[32,1,64]{2,1,0:T(1,128)S(1)} %bitcast.34), channel_id=1, replica_groups=mesh['z'=16,'y'=4,'core'=2,'x'=4] {'y','core','x'}, dimensions={0} | all-to-all | bytes 16384 | tf_op jit(solution)/shard_map/all_to_all | solution.py:343
  112.6 0.1 copy.23
  112.7 0.1 reshape.62
  112.7 16.4 %all_to_all.28 = f32[16,1,128]{2,1,0:T(1,128)S(1)} all-to-all(f32[16,1,128]{2,1,0:T(1,128)S(1)} %bitcast.35), channel_id=1, replica_groups=mesh['z'=16,'y'=4,'core'=2,'x'=4] {'z'}, dimensions={0} | all-to-all | bytes 16384 | tf_op jit(solution)/shard_map/all_to_all | solution.py:345
  129.2 0.9 shard_map.70
  (2 shorter events, 0.0 us)
Async XLA Ops:
  59.8 41.1 %copy-start = (f32[256,768]{1,0:T(8,128)S(1)}, f32[256,768]{1,0:T(8,128)}, u32[]{:S(2)}) copy-start(f32[256,768]{1,0:T(8,128)} %emb_ref.1) | copy-start | bytes 2359300
  59.8 41.1 %copy-start.1 = (s32[512]{0:T(512)S(1)}, s32[512]{0:T(512)}, u32[]{:S(2)}) copy-start(s32[512]{0:T(512)} %param.9) | copy-start | bytes 6148
  59.8 41.1 %copy-start.2 = (s32[256]{0:T(256)S(1)}, s32[256]{0:T(256)}, u32[]{:S(2)}) copy-start(s32[256]{0:T(256)} %param.7) | copy-start | bytes 3076
  59.9 41.1 %copy-start.3 = (s32[256]{0:T(256)S(1)}, s32[256]{0:T(256)}, u32[]{:S(2)}) copy-start(s32[256]{0:T(256)} %param.8) | copy-start | bytes 3076

commit v8 on v6

--- a/solution.py
+++ b/solution.py
@@ -137,9 +137,7 @@
     return lax.dot_general(a, b, NT, preferred_element_type=F32)
 
 
-def slab_pack_kernel(emb_ref, ids_ref, ord_ref, own_ref, out_ref, slot_ref, here_ref, sem):
-    copy = pltpu.make_async_copy(emb_ref, here_ref, sem)
-    copy.start()
+def slab_pack_kernel(emb_ref, ids_ref, ord_ref, own_ref, out_ref, slot_ref):
     target = targets(ids_ref[...], own_ref[...])
     rank = rank_among_equal(target).astype(jnp.int32)
     whole = target.astype(jnp.int32)
@@ -152,13 +150,7 @@
     right = left + jnp.where(place < NQ, NQ, 4)
     left = jnp.where(place < FIT, left, -1)
     right = jnp.where(place < FIT, right, -1)
-    even = hot(iota((128, ROWS), 0) == place)
-    odd = hot(iota((128, ROWS), 0) == place + 64)
-    rows = iota((SENT, ROWS), 0)
-    to_left = hot(rows == left)
-    to_right = hot(rows == right)
-    copy.wait()
-    emb = here_ref[...]
+    emb = emb_ref[...]
     squares = jnp.sum(emb * emb, axis=1, keepdims=True) + 1e-06
     units = (emb * lax.rsqrt(squares)).astype(BF)
     scale = row_of(jnp.sqrt(squares).astype(BF).astype(F32))
@@ -173,13 +165,16 @@
         jnp.where(value == 1, high, jnp.where(value == 2, low, q * 2 + rank + 1)).astype(F32),
     )
     mine = jnp.where(sub - value * NZ == z, picked, 0.0).astype(BF)
+    even = hot(iota((128, ROWS), 0) == place)
+    odd = hot(iota((128, ROWS), 0) == place + 64)
     found = [
         (dot_nt(mine[v * NZ : (v + 1) * NZ], even) + dot_nt(mine[(v + 1) * NZ : (v + 2) * NZ], odd)).astype(BF)
         for v in (0, 2)
     ]
     meta = jnp.concatenate(found + [jnp.broadcast_to(overflow, (NZ, 128)).astype(BF)], axis=1)
+    rows = iota((SENT, ROWS), 0)
     last = hot(iota((SENT, NZ), 0) == iota((SENT, NZ), 1) * CHUNK_Z + 67)
-    sent = dot(to_left, units[:, :HALF]) + dot(to_right, units[:, HALF:])
+    sent = dot(hot(rows == left), units[:, :HALF]) + dot(hot(rows == right), units[:, HALF:])
     out_ref[...] = (sent + dot(last, meta)).astype(BF)
 
 
@@ -317,8 +312,6 @@
         ids_row,
         orders_row,
         owner_row,
-        scratch=[pltpu.VMEM((ROWS, D), F32), pltpu.SemaphoreType.DMA],
-        far=1,
     )
     got = lax.all_to_all(packed.reshape(NZ, CHUNK_Z, HALF), "z", split_axis=0, concat_axis=0, tiled=True)
     (moved,) = call(repack_kernel, [sds((NQ, CHUNK, 128), BF)], got)

time: 130 us -> 130 us (level)
  no operation moved by 1% of the time
where the time goes in v8:
time: 130 us; the launch traced here: 129 us
  blocking collectives  120 us (92%)
  Pallas kernels  8.64 us (7%)
    all_to_all x1, blocking collectives, local(): lax.all_to_all(packed.reshape(NZ, CHUNK_Z, HALF), 'z', split_axis=0, conc...  53.9 us
    all_to_all x1, blocking collectives, local(): rows = lax.all_to_all(moved, SLAB, split_axis=0, concat_axis=0, tiled=True)  38.1 us
    all_to_all x1, blocking collectives, local(): back = lax.all_to_all(back, 'z', split_axis=0, concat_axis=0, tiled=True)  16.4 us
    all_to_all x1, blocking collectives, local(): back = lax.all_to_all(back, SLAB, split_axis=0, concat_axis=0, tiled=True)  11.1 us
    pallas_call x4, Pallas kernels, call(): pl.pallas_call(kernel, out_shape=shapes, scratch_shapes=scratch, compiler...  8.64 us

profile of v8, /device:TPU:1, one launch (start us, length us, event | category | flops | bytes accessed | tf_op | source)
XLA Modules:
  0.0 129.4 jit_solution(9352458521321122601)
XLA Ops:
  0.6 2.8 %shard_map.67 = (bf16[1152,384]{1,0:T(8,128)(2,1)S(1)}, s32[1,256]{1,0:T(1,128)S(1)}) custom-call(f32[256,768]{1,0:T(8,128)} %emb_ref.1, s32[1,256]{1,0:T(1,128)} %bitcast.38, s32[1,256]{1,0:T(1,128)} %bitcast.40, s32[1,512]{1,0:T(1,128)} %bitcast.36), custom_call_target="tpu_custom_call" | custom-call | tf_op jit(solution)/shard_map/pallas_call | solution.py:36
  3.4 53.9 %all_to_all.25.rows_ref = bf16[16,72,384]{2,1,0:T(8,128)(2,1)S(1)} all-to-all(bf16[16,72,384]{2,1,0:T(8,128)(2,1)S(1)} %bitcast.26), channel_id=1, replica_groups=mesh['z'=16,'y'=4,'core'=2,'x'=4] {'z'}, dimensions={0} | all-to-all | bytes 1769472 | tf_op jit(solution)/shard_map/all_to_all | solution.py:316
  57.3 2.0 %shard_map.68 = bf16[32,200,128]{2,1,0:T(8,128)(2,1)S(1)} custom-call(bf16[16,72,384]{2,1,0:T(8,128)(2,1)S(1)} %all_to_all.25.rows_ref), custom_call_target="tpu_custom_call" | custom-call | tf_op jit(solution)/shard_map/pallas_call | solution.py:36
  59.4 0.0 copy-start
  59.4 0.0 copy-start.1
  59.4 0.0 copy-start.2
  59.4 0.0 copy-start.3
  59.4 38.1 %all_to_all.26.rows_ref = bf16[32,200,128]{2,1,0:T(8,128)(2,1)S(1)} all-to-all(bf16[32,200,128]{2,1,0:T(8,128)(2,1)S(1)} %shard_map.68), channel_id=1, replica_groups=mesh['z'=16,'y'=4,'core'=2,'x'=4] {'y','core','x'}, dimensions={0} | all-to-all | bytes 3276800 | tf_op jit(solution)/shard_map/all_to_all | solution.py:318
  97.5 3.0 %shard_map.69 = (f32[1,768]{1,0:T(1,128)}, f32[2,1024]{1,0:T(2,128)S(1)}, f32[1,128]{1,0:T(1,128)S(1)}) custom-call(bf16[32,200,128]{2,1,0:T(8,128)(2,1)S(1)} %all_to_all.26.rows_ref), custom_call_target="tpu_custom_call" | custom-call | tf_op jit(solution)/shard_map/pallas_call | solution.py:36
  100.5 0.0 copy-done
  100.5 0.0 copy-done.1
  100.5 0.0 copy-done.2
  100.5 0.0 copy-done.3
  100.5 0.1 reshape.59
  100.7 0.1 reshape.60
  100.7 11.1 %all_to_all.27 = f32[32,1,64]{2,1,0:T(1,128)S(1)} all-to-all(f32[32,1,64]{2,1,0:T(1,128)S(1)} %bitcast.34), channel_id=1, replica_groups=mesh['z'=16,'y'=4,'core'=2,'x'=4] {'y','core','x'}, dimensions={0} | all-to-all | bytes 16384 | tf_op jit(solution)/shard_map/all_to_all | solution.py:332
  111.9 0.1 copy.23
  112.0 0.1 reshape.62
  112.1 16.4 %all_to_all.28 = f32[16,1,128]{2,1,0:T(1,128)S(1)} all-to-all(f32[16,1,128]{2,1,0:T(1,128)S(1)} %bitcast.35), channel_id=1, replica_groups=mesh['z'=16,'y'=4,'core'=2,'x'=4] {'z'}, dimensions={0} | all-to-all | bytes 16384 | tf_op jit(solution)/shard_map/all_to_all | solution.py:334
  128.5 0.9 shard_map.70
  (3 shorter events, 0.1 us)
Async XLA Ops:
  59.4 41.1 %copy-start = (f32[256,768]{1,0:T(8,128)S(1)}, f32[256,768]{1,0:T(8,128)}, u32[]{:S(2)}) copy-start(f32[256,768]{1,0:T(8,128)} %emb_ref.1) | copy-start | bytes 2359300
  59.4 41.1 %copy-start.1 = (s32[512]{0:T(512)S(1)}, s32[512]{0:T(512)}, u32[]{:S(2)}) copy-start(s32[512]{0:T(512)} %param.9) | copy-start | bytes 6148
  59.4 41.1 %copy-start.2 = (s32[256]{0:T(256)S(1)}, s32[256]{0:T(256)}, u32[]{:S(2)}) copy-start(s32[256]{0:T(256)} %param.7) | copy-start | bytes 3076
  59.4 41.1 %copy-start.3 = (s32[256]{0:T(256)S(1)}, s32[256]{0:T(256)}, u32[]{:S(2)}) copy-start(s32[256]{0:T(256)} %param.8) | copy-start | bytes 3076

commit v9 on v8

--- a/solution.py
+++ b/solution.py
@@ -252,13 +252,29 @@
     length = lax.rsqrt(jnp.sum(center * center, axis=1, keepdims=True) + 1e-06)
     direction = jnp.broadcast_to(center * length, (8, D)).astype(BF)
     back_ref[1:2] = dot_nt(direction, keys_ref[...])[0:1]
+    key_row = jnp.where(values[3:4] > 0.0, order_row, 1e6)
     block = 256
+    best = []
+    across = []
     for b in range(total // block):
-        some = slice(b * block, (b + 1) * block)
-        scores = dot_nt(keys_ref[...], keys_ref[some, :])
-        back_ref[0:1, some] = jnp.max(
-            jnp.where(key_col < order_row[:, some], scores, -1.0), axis=0, keepdims=True
-        )
+        mine = slice(b * block, (b + 1) * block)
+        row = None
+        for a in range(b + 1):
+            other = slice(a * block, (a + 1) * block)
+            scores = dot_nt(keys_ref[other, :], keys_ref[mine, :])
+            found = jnp.where(key_col[other] < order_row[:, mine], scores, -1.0)
+            found = jnp.max(found, axis=0, keepdims=True)
+            row = found if row is None else jnp.maximum(row, found)
+            if a < b:
+                found = jnp.where(key_row[:, mine] < key_col[other], scores, -1.0)
+                found = jnp.max(found, axis=1, keepdims=True)
+                across[a] = found if across[a] is None else jnp.maximum(across[a], found)
+        best.append(row)
+        across.append(None)
+    for b, row in enumerate(best):
+        if across[b] is not None:
+            row = jnp.maximum(row, row_of(across[b]))
+        back_ref[0:1, b * block : (b + 1) * block] = row
 
 
 def unpack_kernel(got_ref, slot_ref, near_ref, align_ref):

time: 130 us -> 129 us (level)
  no operation moved by 1% of the time
where the time goes in v9:
time: 129 us
  blocking collectives  120 us (93%)
  Pallas kernels  8.16 us (6%)
    all_to_all x1, blocking collectives, local(): lax.all_to_all(packed.reshape(NZ, CHUNK_Z, HALF), 'z', split_axis=0, conc...  53.9 us
    all_to_all x1, blocking collectives, local(): rows = lax.all_to_all(moved, SLAB, split_axis=0, concat_axis=0, tiled=True)  38.1 us
    all_to_all x1, blocking collectives, local(): back = lax.all_to_all(back, 'z', split_axis=0, concat_axis=0, tiled=True)  16.4 us
    all_to_all x1, blocking collectives, local(): back = lax.all_to_all(back, SLAB, split_axis=0, concat_axis=0, tiled=True)  11.1 us
    pallas_call x4, Pallas kernels, call(): pl.pallas_call(kernel, out_shape=shapes, scratch_shapes=scratch, compiler...  8.16 us

profile of v9, /device:TPU:1, one launch (start us, length us, event | category | flops | bytes accessed | tf_op | source)
XLA Modules:
  0.0 128.9 jit_solution(16467407039523339943)
XLA Ops:
  0.6 2.8 %shard_map.67 = (bf16[1152,384]{1,0:T(8,128)(2,1)S(1)}, s32[1,256]{1,0:T(1,128)S(1)}) custom-call(f32[256,768]{1,0:T(8,128)} %emb_ref.1, s32[1,256]{1,0:T(1,128)} %bitcast.38, s32[1,256]{1,0:T(1,128)} %bitcast.40, s32[1,512]{1,0:T(1,128)} %bitcast.36), custom_call_target="tpu_custom_call" | custom-call | tf_op jit(solution)/shard_map/pallas_call | solution.py:36
  3.4 53.9 %all_to_all.25.rows_ref = bf16[16,72,384]{2,1,0:T(8,128)(2,1)S(1)} all-to-all(bf16[16,72,384]{2,1,0:T(8,128)(2,1)S(1)} %bitcast.26), channel_id=1, replica_groups=mesh['z'=16,'y'=4,'core'=2,'x'=4] {'z'}, dimensions={0} | all-to-all | bytes 1769472 | tf_op jit(solution)/shard_map/all_to_all | solution.py:332
  57.3 2.0 %shard_map.68 = bf16[32,200,128]{2,1,0:T(8,128)(2,1)S(1)} custom-call(bf16[16,72,384]{2,1,0:T(8,128)(2,1)S(1)} %all_to_all.25.rows_ref), custom_call_target="tpu_custom_call" | custom-call | tf_op jit(solution)/shard_map/pallas_call | solution.py:36
  59.4 0.0 copy-start
  59.4 0.0 copy-start.1
  59.4 0.0 copy-start.2
  59.4 0.0 copy-start.3
  59.4 38.1 %all_to_all.26.rows_ref = bf16[32,200,128]{2,1,0:T(8,128)(2,1)S(1)} all-to-all(bf16[32,200,128]{2,1,0:T(8,128)(2,1)S(1)} %shard_map.68), channel_id=1, replica_groups=mesh['z'=16,'y'=4,'core'=2,'x'=4] {'y','core','x'}, dimensions={0} | all-to-all | bytes 3276800 | tf_op jit(solution)/shard_map/all_to_all | solution.py:334
  97.5 2.5 %shard_map.69 = (f32[1,768]{1,0:T(1,128)}, f32[2,1024]{1,0:T(2,128)S(1)}, f32[1,128]{1,0:T(1,128)S(1)}) custom-call(bf16[32,200,128]{2,1,0:T(8,128)(2,1)S(1)} %all_to_all.26.rows_ref), custom_call_target="tpu_custom_call" | custom-call | tf_op jit(solution)/shard_map/pallas_call | solution.py:36
  100.0 0.0 copy-done
  100.0 0.0 copy-done.1
  100.1 0.0 copy-done.2
  100.1 0.0 copy-done.3
  100.1 0.1 reshape.59
  100.2 0.1 reshape.60
  100.3 11.1 %all_to_all.27 = f32[32,1,64]{2,1,0:T(1,128)S(1)} all-to-all(f32[32,1,64]{2,1,0:T(1,128)S(1)} %bitcast.34), channel_id=1, replica_groups=mesh['z'=16,'y'=4,'core'=2,'x'=4] {'y','core','x'}, dimensions={0} | all-to-all | bytes 16384 | tf_op jit(solution)/shard_map/all_to_all | solution.py:348
  111.4 0.1 copy.23
  111.5 0.1 reshape.62
  111.6 16.4 %all_to_all.28 = f32[16,1,128]{2,1,0:T(1,128)S(1)} all-to-all(f32[16,1,128]{2,1,0:T(1,128)S(1)} %bitcast.35), channel_id=1, replica_groups=mesh['z'=16,'y'=4,'core'=2,'x'=4] {'z'}, dimensions={0} | all-to-all | bytes 16384 | tf_op jit(solution)/shard_map/all_to_all | solution.py:350
  128.0 0.9 shard_map.70
  (3 shorter events, 0.1 us)
Async XLA Ops:
  59.4 40.7 %copy-start = (f32[256,768]{1,0:T(8,128)S(1)}, f32[256,768]{1,0:T(8,128)}, u32[]{:S(2)}) copy-start(f32[256,768]{1,0:T(8,128)} %emb_ref.1) | copy-start | bytes 2359300
  59.4 40.7 %copy-start.1 = (s32[512]{0:T(512)S(1)}, s32[512]{0:T(512)}, u32[]{:S(2)}) copy-start(s32[512]{0:T(512)} %param.9) | copy-start | bytes 6148
  59.4 40.7 %copy-start.2 = (s32[256]{0:T(256)S(1)}, s32[256]{0:T(256)}, u32[]{:S(2)}) copy-start(s32[256]{0:T(256)} %param.7) | copy-start | bytes 3076
  59.4 40.6 %copy-start.3 = (s32[256]{0:T(256)S(1)}, s32[256]{0:T(256)}, u32[]{:S(2)}) copy-start(s32[256]{0:T(256)} %param.8) | copy-start | bytes 3076

commit v10 on v9

--- a/solution.py
+++ b/solution.py
@@ -271,10 +271,13 @@
                 across[a] = found if across[a] is None else jnp.maximum(across[a], found)
         best.append(row)
         across.append(None)
+    lane = iota((block, 128), 1)
+    mirrored = jnp.full((block, 128), -1.0)
+    for a, found in enumerate(across[:-1]):
+        mirrored = jnp.where(lane == a, found, mirrored)
+    mirrored = jnp.transpose(mirrored)
     for b, row in enumerate(best):
-        if across[b] is not None:
-            row = jnp.maximum(row, row_of(across[b]))
-        back_ref[0:1, b * block : (b + 1) * block] = row
+        back_ref[0:1, b * block : (b + 1) * block] = jnp.maximum(row, mirrored[b : b + 1])
 
 
 def unpack_kernel(got_ref, slot_ref, near_ref, align_ref):

time: 129 us -> 129 us (level)
  no operation moved by 1% of the time
where the time goes in v10:
time: 129 us
  blocking collectives  120 us (93%)
  Pallas kernels  8.17 us (6%)
    all_to_all x1, blocking collectives, local(): lax.all_to_all(packed.reshape(NZ, CHUNK_Z, HALF), 'z', split_axis=0, conc...  53.9 us
    all_to_all x1, blocking collectives, local(): rows = lax.all_to_all(moved, SLAB, split_axis=0, concat_axis=0, tiled=True)  38.1 us
    all_to_all x1, blocking collectives, local(): back = lax.all_to_all(back, 'z', split_axis=0, concat_axis=0, tiled=True)  16.4 us
    all_to_all x1, blocking collectives, local(): back = lax.all_to_all(back, SLAB, split_axis=0, concat_axis=0, tiled=True)  11.1 us
    pallas_call x4, Pallas kernels, call(): pl.pallas_call(kernel, out_shape=shapes, scratch_shapes=scratch, compiler...  8.17 us

profile of v10, /device:TPU:1, one launch (start us, length us, event | category | flops | bytes accessed | tf_op | source)
XLA Modules:
  0.0 128.9 jit_solution(2711951532896137123)
XLA Ops:
  0.6 2.8 %shard_map.67 = (bf16[1152,384]{1,0:T(8,128)(2,1)S(1)}, s32[1,256]{1,0:T(1,128)S(1)}) custom-call(f32[256,768]{1,0:T(8,128)} %emb_ref.1, s32[1,256]{1,0:T(1,128)} %bitcast.38, s32[1,256]{1,0:T(1,128)} %bitcast.40, s32[1,512]{1,0:T(1,128)} %bitcast.36), custom_call_target="tpu_custom_call" | custom-call | tf_op jit(solution)/shard_map/pallas_call | solution.py:36
  3.4 53.9 %all_to_all.25.rows_ref = bf16[16,72,384]{2,1,0:T(8,128)(2,1)S(1)} all-to-all(bf16[16,72,384]{2,1,0:T(8,128)(2,1)S(1)} %bitcast.26), channel_id=1, replica_groups=mesh['z'=16,'y'=4,'core'=2,'x'=4] {'z'}, dimensions={0} | all-to-all | bytes 1769472 | tf_op jit(solution)/shard_map/all_to_all | solution.py:335
  57.3 2.0 %shard_map.68 = bf16[32,200,128]{2,1,0:T(8,128)(2,1)S(1)} custom-call(bf16[16,72,384]{2,1,0:T(8,128)(2,1)S(1)} %all_to_all.25.rows_ref), custom_call_target="tpu_custom_call" | custom-call | tf_op jit(solution)/shard_map/pallas_call | solution.py:36
  59.4 0.0 copy-start
  59.4 0.0 copy-start.1
  59.4 0.0 copy-start.2
  59.4 0.0 copy-start.3
  59.4 38.1 %all_to_all.26.rows_ref = bf16[32,200,128]{2,1,0:T(8,128)(2,1)S(1)} all-to-all(bf16[32,200,128]{2,1,0:T(8,128)(2,1)S(1)} %shard_map.68), channel_id=1, replica_groups=mesh['z'=16,'y'=4,'core'=2,'x'=4] {'y','core','x'}, dimensions={0} | all-to-all | bytes 3276800 | tf_op jit(solution)/shard_map/all_to_all | solution.py:337
  97.5 2.5 %shard_map.69 = (f32[1,768]{1,0:T(1,128)}, f32[2,1024]{1,0:T(2,128)S(1)}, f32[1,128]{1,0:T(1,128)S(1)}) custom-call(bf16[32,200,128]{2,1,0:T(8,128)(2,1)S(1)} %all_to_all.26.rows_ref), custom_call_target="tpu_custom_call" | custom-call | tf_op jit(solution)/shard_map/pallas_call | solution.py:36
  100.0 0.0 copy-done
  100.0 0.0 copy-done.1
  100.1 0.0 copy-done.2
  100.1 0.0 copy-done.3
  100.1 0.1 reshape.59
  100.2 0.1 reshape.60
  100.3 11.1 %all_to_all.27 = f32[32,1,64]{2,1,0:T(1,128)S(1)} all-to-all(f32[32,1,64]{2,1,0:T(1,128)S(1)} %bitcast.34), channel_id=1, replica_groups=mesh['z'=16,'y'=4,'core'=2,'x'=4] {'y','core','x'}, dimensions={0} | all-to-all | bytes 16384 | tf_op jit(solution)/shard_map/all_to_all | solution.py:351
  111.4 0.1 copy.23
  111.5 0.1 reshape.62
  111.6 16.4 %all_to_all.28 = f32[16,1,128]{2,1,0:T(1,128)S(1)} all-to-all(f32[16,1,128]{2,1,0:T(1,128)S(1)} %bitcast.35), channel_id=1, replica_groups=mesh['z'=16,'y'=4,'core'=2,'x'=4] {'z'}, dimensions={0} | all-to-all | bytes 16384 | tf_op jit(solution)/shard_map/all_to_all | solution.py:353
  128.0 0.9 shard_map.70
  (3 shorter events, 0.1 us)
Async XLA Ops:
  59.4 40.7 %copy-start = (f32[256,768]{1,0:T(8,128)S(1)}, f32[256,768]{1,0:T(8,128)}, u32[]{:S(2)}) copy-start(f32[256,768]{1,0:T(8,128)} %emb_ref.1) | copy-start | bytes 2359300
  59.4 40.7 %copy-start.1 = (s32[512]{0:T(512)S(1)}, s32[512]{0:T(512)}, u32[]{:S(2)}) copy-start(s32[512]{0:T(512)} %param.9) | copy-start | bytes 6148
  59.4 40.7 %copy-start.2 = (s32[256]{0:T(256)S(1)}, s32[256]{0:T(256)}, u32[]{:S(2)}) copy-start(s32[256]{0:T(256)} %param.7) | copy-start | bytes 3076
  59.4 40.7 %copy-start.3 = (s32[256]{0:T(256)S(1)}, s32[256]{0:T(256)}, u32[]{:S(2)}) copy-start(s32[256]{0:T(256)} %param.8) | copy-start | bytes 3076

commit v11 on v10

--- a/solution.py
+++ b/solution.py
@@ -246,12 +246,6 @@
     order_row = values[1:2] * 256.0 + values[2:3]
     members = jnp.sum(values[3:4], axis=1, keepdims=True)
     key_col = column(jnp.where(values[3:4] > 0.0, order_row, 1e6))
-    scale = jnp.broadcast_to(values[0:1], (8, total)).astype(BF)
-    center = dot(scale, keys_ref[...])[0:1] / members
-    center_ref[...] = center
-    length = lax.rsqrt(jnp.sum(center * center, axis=1, keepdims=True) + 1e-06)
-    direction = jnp.broadcast_to(center * length, (8, D)).astype(BF)
-    back_ref[1:2] = dot_nt(direction, keys_ref[...])[0:1]
     key_row = jnp.where(values[3:4] > 0.0, order_row, 1e6)
     block = 256
     best = []
@@ -278,6 +272,12 @@
     mirrored = jnp.transpose(mirrored)
     for b, row in enumerate(best):
         back_ref[0:1, b * block : (b + 1) * block] = jnp.maximum(row, mirrored[b : b + 1])
+    scale = jnp.broadcast_to(values[0:1], (8, total)).astype(BF)
+    center = dot(scale, keys_ref[...])[0:1] / members
+    center_ref[...] = center
+    length = lax.rsqrt(jnp.sum(center * center, axis=1, keepdims=True) + 1e-06)
+    direction = jnp.broadcast_to(center * length, (8, D)).astype(BF)
+    back_ref[1:2] = dot_nt(direction, keys_ref[...])[0:1]
 
 
 def unpack_kernel(got_ref, slot_ref, near_ref, align_ref):

time: 129 us -> 129 us (level)
  no operation moved by 1% of the time
where the time goes in v11:
time: 129 us
  blocking collectives  120 us (93%)
  Pallas kernels  7.76 us (6%)
    all_to_all x1, blocking collectives, local(): lax.all_to_all(packed.reshape(NZ, CHUNK_Z, HALF), 'z', split_axis=0, conc...  53.9 us
    all_to_all x1, blocking collectives, local(): rows = lax.all_to_all(moved, SLAB, split_axis=0, concat_axis=0, tiled=True)  38.1 us
    all_to_all x1, blocking collectives, local(): back = lax.all_to_all(back, 'z', split_axis=0, concat_axis=0, tiled=True)  16.4 us
    all_to_all x1, blocking collectives, local(): back = lax.all_to_all(back, SLAB, split_axis=0, concat_axis=0, tiled=True)  11.1 us
    pallas_call x4, Pallas kernels, call(): pl.pallas_call(kernel, out_shape=shapes, scratch_shapes=scratch, compiler...  7.76 us

profile of v11, /device:TPU:1, one launch (start us, length us, event | category | flops | bytes accessed | tf_op | source)
XLA Modules:
  0.0 128.5 jit_solution(2724027746056305963)
XLA Ops:
  0.6 2.8 %shard_map.67 = (bf16[1152,384]{1,0:T(8,128)(2,1)S(1)}, s32[1,256]{1,0:T(1,128)S(1)}) custom-call(f32[256,768]{1,0:T(8,128)} %emb_ref.1, s32[1,256]{1,0:T(1,128)} %bitcast.38, s32[1,256]{1,0:T(1,128)} %bitcast.40, s32[1,512]{1,0:T(1,128)} %bitcast.36), custom_call_target="tpu_custom_call" | custom-call | tf_op jit(solution)/shard_map/pallas_call | solution.py:36
  3.4 53.9 %all_to_all.25.rows_ref = bf16[16,72,384]{2,1,0:T(8,128)(2,1)S(1)} all-to-all(bf16[16,72,384]{2,1,0:T(8,128)(2,1)S(1)} %bitcast.26), channel_id=1, replica_groups=mesh['z'=16,'y'=4,'core'=2,'x'=4] {'z'}, dimensions={0} | all-to-all | bytes 1769472 | tf_op jit(solution)/shard_map/all_to_all | solution.py:335
  57.3 2.0 %shard_map.68 = bf16[32,200,128]{2,1,0:T(8,128)(2,1)S(1)} custom-call(bf16[16,72,384]{2,1,0:T(8,128)(2,1)S(1)} %all_to_all.25.rows_ref), custom_call_target="tpu_custom_call" | custom-call | tf_op jit(solution)/shard_map/pallas_call | solution.py:36
  59.4 0.0 copy-start
  59.4 0.0 copy-start.1
  59.4 0.0 copy-start.2
  59.4 0.0 copy-start.3
  59.4 38.1 %all_to_all.26.rows_ref = bf16[32,200,128]{2,1,0:T(8,128)(2,1)S(1)} all-to-all(bf16[32,200,128]{2,1,0:T(8,128)(2,1)S(1)} %shard_map.68), channel_id=1, replica_groups=mesh['z'=16,'y'=4,'core'=2,'x'=4] {'y','core','x'}, dimensions={0} | all-to-all | bytes 3276800 | tf_op jit(solution)/shard_map/all_to_all | solution.py:337
  97.5 2.1 %shard_map.69 = (f32[1,768]{1,0:T(1,128)}, f32[2,1024]{1,0:T(2,128)S(1)}, f32[1,128]{1,0:T(1,128)S(1)}) custom-call(bf16[32,200,128]{2,1,0:T(8,128)(2,1)S(1)} %all_to_all.26.rows_ref), custom_call_target="tpu_custom_call" | custom-call | tf_op jit(solution)/shard_map/pallas_call | solution.py:36
  99.6 0.0 copy-done
  99.6 0.0 copy-done.1
  99.6 0.0 copy-done.2
  99.6 0.0 copy-done.3
  99.7 0.1 reshape.59
  99.8 0.1 reshape.60
  99.9 11.1 %all_to_all.27 = f32[32,1,64]{2,1,0:T(1,128)S(1)} all-to-all(f32[32,1,64]{2,1,0:T(1,128)S(1)} %bitcast.34), channel_id=1, replica_groups=mesh['z'=16,'y'=4,'core'=2,'x'=4] {'y','core','x'}, dimensions={0} | all-to-all | bytes 16384 | tf_op jit(solution)/shard_map/all_to_all | solution.py:351
  111.0 0.1 copy.23
  111.1 0.1 reshape.62
  111.2 16.4 %all_to_all.28 = f32[16,1,128]{2,1,0:T(1,128)S(1)} all-to-all(f32[16,1,128]{2,1,0:T(1,128)S(1)} %bitcast.35), channel_id=1, replica_groups=mesh['z'=16,'y'=4,'core'=2,'x'=4] {'z'}, dimensions={0} | all-to-all | bytes 16384 | tf_op jit(solution)/shard_map/all_to_all | solution.py:353
  127.6 0.9 shard_map.70
  (3 shorter events, 0.1 us)
Async XLA Ops:
  59.4 40.2 %copy-start = (f32[256,768]{1,0:T(8,128)S(1)}, f32[256,768]{1,0:T(8,128)}, u32[]{:S(2)}) copy-start(f32[256,768]{1,0:T(8,128)} %emb_ref.1) | copy-start | bytes 2359300
  59.4 40.2 %copy-start.1 = (s32[512]{0:T(512)S(1)}, s32[512]{0:T(512)}, u32[]{:S(2)}) copy-start(s32[512]{0:T(512)} %param.9) | copy-start | bytes 6148
  59.4 40.2 %copy-start.2 = (s32[256]{0:T(256)S(1)}, s32[256]{0:T(256)}, u32[]{:S(2)}) copy-start(s32[256]{0:T(256)} %param.7) | copy-start | bytes 3076
  59.4 40.2 %copy-start.3 = (s32[256]{0:T(256)S(1)}, s32[256]{0:T(256)}, u32[]{:S(2)}) copy-start(s32[256]{0:T(256)} %param.8) | copy-start | bytes 3076
